TPU v7x, 32 devices: a whole 2x2x4 slice. The times are simulated.
32 devices in a mesh: groups: 2 (over x), tiles: 16 (over z, y, core).
Axes of the slice: x: 2, y: 2, z: 4, core: 2. Of those that a mesh axis runs over, the one named last changes fastest.
Arguments:
- features: bfloat16 [512, 128, 128], P(('groups', 'tiles')), parts along dimension 0, may hold values from -40 to 40
- window_offsets: int32 [4], P('groups'), parts along dimension 0, may hold values from 0 to 31
- self_project: bfloat16 [128, 384], replicated, may hold values from -0.5 to 0.5
- self_merge: bfloat16 [128, 128], replicated, may hold values from -0.5 to 0.5
- cross_project: bfloat16 [128, 384], replicated, may hold values from -0.5 to 0.5
- cross_merge: bfloat16 [128, 128], replicated, may hold values from -0.5 to 0.5
- feed_in: bfloat16 [256, 512], replicated, may hold values from -0.375 to 0.375
- feed_out: bfloat16 [512, 128], replicated, may hold values from -0.25 to 0.25
- norm_gains: float32 [3, 128], replicated, may hold values from 0.1 to 1.9
- result_grad: float32 [512, 128, 128], P(('groups', 'tiles')), parts along dimension 0, may hold values from -6 to 6
Outputs:
- result: bfloat16 [512, 128, 128], P(('groups', 'tiles')), parts along dimension 0
- features_grad: float32 [512, 128, 128], P(('groups', 'tiles')), parts along dimension 0
- self_project_grad: float32 [256, 384], P(('groups', 'tiles')), parts along dimension 0
- self_merge_grad: float32 [256, 128], P(('groups', 'tiles')), parts along dimension 0
- cross_project_grad: float32 [256, 384], P(('groups', 'tiles')), parts along dimension 0
- cross_merge_grad: float32 [256, 128], P(('groups', 'tiles')), parts along dimension 0
- feed_in_grad: float32 [512, 512], P(('groups', 'tiles')), parts along dimension 0
- feed_out_grad: float32 [1024, 128], P(('groups', 'tiles')), parts along dimension 0
- norm_gains_grad: float32 [6, 128], P('groups', 'tiles'), parts along dimension 0
There are 2 independent parts, one for each index of `groups`. A program takes and returns all parts, laid end to end along the dimension named above; an argument that names none is the same for every part. Nothing has to cross between parts.
All inputs are finite; a program needn't handle non-finite values.
Results may differ from a plain program's by a relative error of at most 0.017.
The roundings to bfloat16 on the way count: a program that leaves them out, or rounds other values in their place, can miss the bound.
Values may be sent and summed in bfloat16 or wider, within the bound.
No kernel may reach another device: no remote copies, remote signals or barrier semaphores. Data moves between devices by JAX's collectives and lax.ppermute only.
A program may use at most 128 MiB of HBM per device.

v0:
```python
import functools
import math

import jax
import jax.numpy as jnp
from jax import lax
from jax.experimental import pallas as pl
from jax.experimental.pallas import tpu as pltpu
from jax.sharding import PartitionSpec as P


D = 128
WIN = 32

NORM_EPS = 1e-05
MASK_FILL = -1000000000.0
HALF_ROOT = 0.7071067811865476
DENSITY_COEF = 0.3989422804014327
LOG2_E = 1.4426950408889634
SCALE = D ** (-0.5)


F32 = jnp.float32
BF16 = jnp.bfloat16


def dot_nn(a, b):
    return lax.dot_general(a, b, (((1,), (0,)), ((), ())), preferred_element_type=F32)


def dot_nt(a, b):
    return lax.dot_general(a, b, (((1,), (1,)), ((), ())), preferred_element_type=F32)


def dot_tn(a, b):
    return lax.dot_general(a, b, (((0,), (0,)), ((), ())), preferred_element_type=F32)


def layer_norm(values, gain):
    center = values - jnp.mean(values, axis=-1, keepdims=True)
    inverse = lax.rsqrt(jnp.mean(center * center, axis=-1, keepdims=True) + NORM_EPS)
    unit = center * inverse
    return unit * gain, unit, inverse


def norm_backward(upstream, gain, unit, inverse):
    scaled = upstream * gain
    grad = inverse * (
        scaled
        - jnp.mean(scaled, axis=-1, keepdims=True)
        - unit * jnp.mean(scaled * unit, axis=-1, keepdims=True)
    )
    return grad, jnp.sum(upstream * unit, axis=0, keepdims=True)


def roll_matrices(offset, size):
    i = lax.broadcasted_iota(jnp.int32, (size, size), 0)
    j = lax.broadcasted_iota(jnp.int32, (size, size), 1)
    row_source = i + offset
    row_source = jnp.where(row_source >= size, row_source - size, row_source)
    col_source = j + offset
    col_source = jnp.where(col_source >= size, col_source - size, col_source)
    forward = jnp.where(j == row_source, 1.0, 0.0).astype(BF16)
    back = jnp.where(i == col_source, 1.0, 0.0).astype(BF16)
    return forward, back


def pick(ref, cols, lanes):
    block = ref[:, cols, lanes]
    return block.reshape(block.shape[0] * block.shape[1], block.shape[2])


def self_forward_kernel(
    scal_ref, own_ref, halo_ref, project_ref, merge_ref, gains_ref,
    middle_ref, mix_ref, qkv_ref, halo_kv_ref, own_rolled, halo_rolled, mix_rolled,
    *, valid_slot,
):
    rows, cols = own_ref.shape[0], own_ref.shape[1]
    forward, back = roll_matrices(scal_ref[0], cols)
    valid = scal_ref[valid_slot] > 0
    for r in range(rows):
        own_rolled[r] = dot_nn(forward, own_ref[r]).astype(BF16)
        halo_rolled[r] = dot_nn(forward, halo_ref[r]).astype(BF16)
    tokens = rows * cols
    qkv_ref[...] = (
        dot_nn(own_rolled[...].reshape(tokens, D), project_ref[...])
        .astype(BF16).reshape(rows, cols, 3 * D)
    )
    halo_kv_ref[...] = (
        dot_nn(halo_rolled[...].reshape(tokens, D), project_ref[:, D:])
        .astype(BF16).reshape(rows, cols, 2 * D)
    )
    for w in range(cols // WIN):
        span = slice(w * WIN, (w + 1) * WIN)
        q = pick(qkv_ref, span, slice(0, D))
        s_own = dot_nt(q, pick(qkv_ref, span, slice(D, 2 * D))) * SCALE
        s_halo = dot_nt(q, pick(halo_kv_ref, span, slice(0, D))) * SCALE
        s_halo = jnp.where(valid, s_halo, MASK_FILL)
        top = jnp.maximum(
            jnp.max(s_own, axis=-1, keepdims=True), jnp.max(s_halo, axis=-1, keepdims=True)
        )
        p_own = jnp.exp(s_own - top)
        p_halo = jnp.exp(s_halo - top)
        inv = 1.0 / (
            jnp.sum(p_own, axis=-1, keepdims=True) + jnp.sum(p_halo, axis=-1, keepdims=True)
        )
        mixed = dot_nn(
            (p_own * inv).astype(BF16), pick(qkv_ref, span, slice(2 * D, 3 * D))
        ) + dot_nn((p_halo * inv).astype(BF16), pick(halo_kv_ref, span, slice(D, 2 * D)))
        mix_rolled[:, span, :] = mixed.astype(BF16).reshape(rows, WIN, D)
    for r in range(rows):
        mix_ref[r * cols : (r + 1) * cols, :] = dot_nn(back, mix_rolled[r]).astype(BF16)
    normed, _, _ = layer_norm(dot_nn(mix_ref[...], merge_ref[...]), gains_ref[0:1, :])
    middle_ref[...] = (own_ref[...].reshape(tokens, D).astype(F32) + normed).astype(BF16)


def full_spec(shape):
    zeros = (0,) * len(shape)
    return pl.BlockSpec(shape, lambda *_: zeros)


def self_forward(group, scal, features, halo, self_project, self_merge, norm_gains):
    rows, cols, _ = halo.shape
    tokens = rows * cols
    return pl.pallas_call(
        functools.partial(self_forward_kernel, valid_slot=1 + group),
        grid=(1,),
        in_specs=[
            pl.BlockSpec(memory_space=pltpu.SMEM),
            pl.BlockSpec((rows, cols, D), lambda i: (group, 0, 0)),
            full_spec(halo.shape),
            full_spec(self_project.shape),
            full_spec(self_merge.shape),
            full_spec(norm_gains.shape),
        ],
        out_specs=[
            full_spec((tokens, D)),
            full_spec((tokens, D)),
            full_spec((rows, cols, 3 * D)),
            full_spec((rows, cols, 2 * D)),
        ],
        out_shape=[
            jax.ShapeDtypeStruct((tokens, D), BF16),
            jax.ShapeDtypeStruct((tokens, D), BF16),
            jax.ShapeDtypeStruct((rows, cols, 3 * D), BF16),
            jax.ShapeDtypeStruct((rows, cols, 2 * D), BF16),
        ],
        scratch_shapes=[pltpu.VMEM((rows, cols, D), BF16)] * 3,
        name="self_forward",
    )(scal, features, halo, self_project, self_merge, norm_gains)


def cross_open_kernel(middle_ref, partner_ref, project_ref, q_ref, kv_ref, mix_ref, stat_ref):
    @pl.when(pl.program_id(0) == 0)
    def _():
        kv_ref[...] = dot_nn(partner_ref[...], project_ref[:, D:]).astype(BF16)

    q = dot_nn(middle_ref[...], project_ref[:, :D]).astype(BF16)
    q_ref[...] = q
    logits = dot_nt(q, kv_ref[:, :D]) * (SCALE * LOG2_E)
    top = jnp.max(logits, axis=-1, keepdims=True)
    raised = jnp.exp2(logits - top)
    total = jnp.sum(raised, axis=-1, keepdims=True)
    mix_ref[...] = dot_nn(raised.astype(BF16), kv_ref[:, D:])
    lane = lax.broadcasted_iota(jnp.int32, stat_ref.shape, 1)
    stat_ref[...] = jnp.where(lane == 0, top, total)


def cross_open(block, middles, partner, cross_project):
    chunk = partner.shape[0]
    tokens = middles.shape[0]
    row = lambda i: (i, 0)
    return pl.pallas_call(
        cross_open_kernel,
        grid=(tokens // block,),
        in_specs=[
            pl.BlockSpec((block, D), row),
            full_spec(partner.shape),
            full_spec(cross_project.shape),
        ],
        out_specs=[
            pl.BlockSpec((block, D), row),
            full_spec((chunk, 2 * D)),
            pl.BlockSpec((block, D), row),
            pl.BlockSpec((block, D), row),
        ],
        out_shape=[
            jax.ShapeDtypeStruct((tokens, D), BF16),
            jax.ShapeDtypeStruct((chunk, 2 * D), BF16),
            jax.ShapeDtypeStruct((tokens, D), F32),
            jax.ShapeDtypeStruct((tokens, D), F32),
        ],
        name="cross_open",
    )(middles, partner, cross_project)


def cross_close_kernel(
    middle_ref, partner_ref, project_ref, q_ref, open_mix_ref, open_stat_ref,
    merge_ref, feed_in_ref, feed_out_ref, gains_ref, upstream_ref,
    kv_ref, result_ref, mid_grad_ref, mix_grad_ref, stat_ref,
    grad_in_ref, grad_out_ref, grad_merge_ref, grad_gain_ref,
):
    @pl.when(pl.program_id(0) == 0)
    def _():
        kv_ref[...] = dot_nn(partner_ref[...], project_ref[:, D:]).astype(BF16)
        grad_in_ref[...] = jnp.zeros_like(grad_in_ref)
        grad_out_ref[...] = jnp.zeros_like(grad_out_ref)
        grad_merge_ref[...] = jnp.zeros_like(grad_merge_ref)
        grad_gain_ref[...] = jnp.zeros_like(grad_gain_ref)

    block = middle_ref.shape[0]
    logits = dot_nt(q_ref[...], kv_ref[:, :D]) * (SCALE * LOG2_E)
    open_top = open_stat_ref[:, 0:1]
    open_total = open_stat_ref[:, 1:2]
    top = jnp.maximum(jnp.max(logits, axis=-1, keepdims=True), open_top)
    raised = jnp.exp2(logits - top)
    carry = jnp.exp2(open_top - top)
    total = jnp.sum(raised, axis=-1, keepdims=True) + open_total * carry
    mixed = dot_nn(raised.astype(BF16), kv_ref[:, D:]) + open_mix_ref[...] * carry
    mixed = mixed * (1.0 / total)
    log_total = top + jnp.log2(total)
    cross_mix = mixed.astype(BF16)

    middle = middle_ref[...]
    gain_cross = gains_ref[1:2, :]
    gain_feed = gains_ref[2:3, :]
    cross_full, cross_unit, cross_inverse = layer_norm(
        dot_nn(cross_mix, merge_ref[...]), gain_cross
    )
    cross_normed = cross_full.astype(BF16)
    feed_pre = dot_nn(middle, feed_in_ref[:D, :]) + dot_nn(cross_normed, feed_in_ref[D:, :])
    bell = 0.5 * (1.0 + lax.erf(feed_pre * HALF_ROOT))
    hidden = (feed_pre * bell).astype(BF16)
    slope = bell + feed_pre * (jnp.exp(-0.5 * feed_pre * feed_pre) * DENSITY_COEF)
    feed_normed, feed_unit, feed_inverse = layer_norm(
        dot_nn(hidden, feed_out_ref[...]), gain_feed
    )
    result_ref[...] = (middle.astype(F32) + feed_normed).astype(BF16)
    upstream = upstream_ref[...]
    post_full, gain_grad_feed = norm_backward(upstream, gain_feed, feed_unit, feed_inverse)
    grad_post = post_full.astype(BF16)
    grad_pre = (dot_nt(grad_post, feed_out_ref[...]) * slope).astype(BF16)
    grad_joined = dot_nt(grad_pre, feed_in_ref[...])
    mid_grad_ref[...] = upstream + grad_joined[:, :D]
    lanes = grad_in_ref.shape[0]
    grad_low = dot_tn(middle, grad_pre)
    grad_high = dot_tn(cross_normed, grad_pre)
    for b in range(lanes):
        grad_in_ref[b, :D, :] += grad_low[:, b * D : (b + 1) * D]
        grad_in_ref[b, D:, :] += grad_high[:, b * D : (b + 1) * D]
    grad_out_ref[...] += dot_tn(hidden, grad_post)
    merged_full, gain_grad_cross = norm_backward(
        grad_joined[:, D:], gain_cross, cross_unit, cross_inverse
    )
    grad_merged = merged_full.astype(BF16)
    grad_merge_ref[...] += dot_tn(cross_mix, grad_merged)
    mix_grad = dot_nt(grad_merged, merge_ref[...]).astype(BF16)
    mix_grad_ref[...] = mix_grad
    inner = jnp.sum(mix_grad.astype(F32) * mixed, axis=-1, keepdims=True)
    lane = lax.broadcasted_iota(jnp.int32, (block, D), 1)
    stats = jnp.where(lane == 0, log_total, inner)
    stat_ref[...] = stats.T[: stat_ref.shape[0], :]
    grad_gain_ref[1:2, :] += gain_grad_cross
    grad_gain_ref[2:3, :] += gain_grad_feed


def cross_close(
    block, middles, partner, cross_project, q, open_mix, open_stat,
    cross_merge, feed_in, feed_out, norm_gains, upstream,
):
    tokens = middles.shape[0]
    chunk = partner.shape[0]
    hidden = feed_in.shape[1]
    row = lambda i: (i, 0)
    tile = pl.BlockSpec((block, D), row)
    return pl.pallas_call(
        cross_close_kernel,
        grid=(tokens // block,),
        in_specs=[
            tile, full_spec(partner.shape), full_spec(cross_project.shape), tile, tile, tile,
            full_spec(cross_merge.shape), full_spec(feed_in.shape), full_spec(feed_out.shape),
            full_spec(norm_gains.shape), tile,
        ],
        out_specs=[
            full_spec((chunk, 2 * D)), tile, tile, tile,
            pl.BlockSpec((8, block), lambda i: (0, i)),
            full_spec((hidden // D, 2 * D, D)), full_spec((hidden, D)), full_spec((D, D)),
            full_spec((8, D)),
        ],
        out_shape=[
            jax.ShapeDtypeStruct((chunk, 2 * D), BF16),
            jax.ShapeDtypeStruct((tokens, D), BF16),
            jax.ShapeDtypeStruct((tokens, D), F32),
            jax.ShapeDtypeStruct((tokens, D), BF16),
            jax.ShapeDtypeStruct((8, tokens), F32),
            jax.ShapeDtypeStruct((hidden // D, 2 * D, D), F32),
            jax.ShapeDtypeStruct((hidden, D), F32),
            jax.ShapeDtypeStruct((D, D), F32),
            jax.ShapeDtypeStruct((8, D), F32),
        ],
        name="cross_close",
    )(middles, partner, cross_project, q, open_mix, open_stat,
      cross_merge, feed_in, feed_out, norm_gains, upstream)


def cross_back_kernel(*refs, first, last, q_block):
    refs = list(refs)
    q_ref, grad_ref, stat_ref, kv_ref, partner_ref, project_ref = refs[:6]
    refs = refs[6:]
    if not first:
        q_in_ref, weight_in_ref = refs[:2]
        refs = refs[2:]
    if last:
        mid_grad_ref, middle_ref = refs[:2]
        refs = refs[2:]
    term_ref, q_out_ref, weight_ref, k_acc, v_acc, q_acc = refs
    step = pl.program_id(0)

    @pl.when(step == 0)
    def _():
        if first:
            q_acc[...] = jnp.zeros_like(q_acc)
            weight_ref[...] = jnp.zeros_like(weight_ref)
        else:
            q_acc[...] = q_in_ref[...]
            weight_ref[...] = weight_in_ref[...]

    k_acc[...] = jnp.zeros_like(k_acc)
    v_acc[...] = jnp.zeros_like(v_acc)
    keys = kv_ref[:, :D]
    values = kv_ref[:, D:]
    tokens = q_ref.shape[0]

    @pl.loop(0, tokens // q_block)
    def _(j):
        span = pl.ds(pl.multiple_of(j * q_block, q_block), q_block)
        q = q_ref[span, :]
        grad = grad_ref[span, :]
        log_total = stat_ref[0:1, span]
        inner = stat_ref[1:2, span]
        shares = jnp.exp2(dot_nt(keys, q) * (SCALE * LOG2_E) - log_total)
        slopes = dot_nt(values, grad) - inner
        v_acc[...] += dot_nn(shares.astype(BF16), grad)
        logit_grad = (shares * slopes).astype(BF16)
        k_acc[...] += dot_nn(logit_grad, q)
        q_acc[span, :] += dot_tn(logit_grad, keys)

    pair = jnp.concatenate(
        [(k_acc[...] * SCALE).astype(BF16), v_acc[...].astype(BF16)], axis=1
    )
    term_ref[...] = dot_nt(pair, project_ref[:, D:]).astype(BF16)
    pair_weight = dot_tn(partner_ref[...], pair)
    weight_ref[1] += pair_weight[:, :D]
    weight_ref[2] += pair_weight[:, D:]

    @pl.when(step == pl.num_programs(0) - 1)
    def _():
        if last:
            q_grad = (q_acc[...] * SCALE).astype(BF16)
            q_out_ref[...] = mid_grad_ref[...] + dot_nt(q_grad, project_ref[:, :D])
            weight_ref[0] += dot_tn(middle_ref[...], q_grad)
        else:
            q_out_ref[...] = q_acc[...]


def cross_back(
    block, index, q_block, q, mix_grad, stats, kv, partner, cross_project,
    carried=None, finish=None,
):
    tokens = q.shape[0]
    first, last = carried is None, finish is not None
    args = [q, mix_grad, stats, kv, partner, cross_project]
    specs = [
        full_spec(q.shape), full_spec(mix_grad.shape), full_spec(stats.shape),
        pl.BlockSpec((block, 2 * D), lambda i: (index, 0)),
        pl.BlockSpec((block, D), lambda i: (index, 0)),
        full_spec(cross_project.shape),
    ]
    for extra in (carried or ()) + (finish or ()):
        args.append(extra)
        specs.append(full_spec(extra.shape))
    return pl.pallas_call(
        functools.partial(cross_back_kernel, first=first, last=last, q_block=q_block),
        grid=(1,),
        in_specs=specs,
        out_specs=[
            full_spec((block, D)), full_spec((tokens, D)), full_spec((3, D, D)),
        ],
        out_shape=[
            jax.ShapeDtypeStruct((block, D), BF16),
            jax.ShapeDtypeStruct((tokens, D), F32),
            jax.ShapeDtypeStruct((3, D, D), F32),
        ],
        scratch_shapes=[
            pltpu.VMEM((block, D), F32), pltpu.VMEM((block, D), F32), pltpu.VMEM((tokens, D), F32)
        ],
        name="cross_back",
    )(*args)


def self_back_kernel(
    scal_ref, own_ref, halo_ref, qkv_ref, halo_kv_ref, mix_ref, mid_grad_ref,
    term_low_ref, term_high_ref, project_ref, merge_ref, gains_ref,
    feature_grad_ref, halo_term_ref, weight_ref, merge_grad_ref, gain_ref,
    mix_grad, own_grad, halo_grad, own_back, halo_back,
    *, valid_slot,
):
    rows, cols = own_ref.shape[0], own_ref.shape[1]
    tokens = rows * cols
    forward, back = roll_matrices(scal_ref[0], cols)
    valid = scal_ref[valid_slot] > 0
    upstream = mid_grad_ref[...] + jnp.concatenate(
        [term_low_ref[...].astype(F32), term_high_ref[...].astype(F32)], axis=0
    )
    gain = gains_ref[0:1, :]
    _, unit, inverse = layer_norm(dot_nn(mix_ref[...], merge_ref[...]), gain)
    merged_full, gain_grad = norm_backward(upstream, gain, unit, inverse)
    gain_ref[...] = jnp.broadcast_to(gain_grad, gain_ref.shape)
    grad_merged = merged_full.astype(BF16)
    merge_grad_ref[...] = dot_tn(mix_ref[...], grad_merged)
    plain_grad = dot_nt(grad_merged, merge_ref[...]).astype(BF16)
    for r in range(rows):
        mix_grad[r] = dot_nn(forward, plain_grad[r * cols : (r + 1) * cols, :]).astype(BF16)
    for w in range(cols // WIN):
        span = slice(w * WIN, (w + 1) * WIN)
        q = pick(qkv_ref, span, slice(0, D))
        k_own = pick(qkv_ref, span, slice(D, 2 * D))
        k_halo = pick(halo_kv_ref, span, slice(0, D))
        grad = pick(mix_grad, span, slice(0, D))
        s_own = dot_nt(k_own, q) * SCALE
        s_halo = jnp.where(valid, dot_nt(k_halo, q) * SCALE, MASK_FILL)
        top = jnp.maximum(
            jnp.max(s_own, axis=0, keepdims=True), jnp.max(s_halo, axis=0, keepdims=True)
        )
        p_own = jnp.exp(s_own - top)
        p_halo = jnp.exp(s_halo - top)
        inv = 1.0 / (
            jnp.sum(p_own, axis=0, keepdims=True) + jnp.sum(p_halo, axis=0, keepdims=True)
        )
        p_own = p_own * inv
        p_halo = p_halo * inv
        d_own = dot_nt(pick(qkv_ref, span, slice(2 * D, 3 * D)), grad)
        d_halo = dot_nt(pick(halo_kv_ref, span, slice(D, 2 * D)), grad)
        inner = jnp.sum(p_own * d_own, axis=0, keepdims=True) + jnp.sum(
            p_halo * d_halo, axis=0, keepdims=True
        )
        l_own = (p_own * (d_own - inner) * SCALE).astype(BF16)
        l_halo = (p_halo * (d_halo - inner) * SCALE).astype(BF16)
        q_grad = dot_tn(l_own, k_own) + dot_tn(l_halo, k_halo)
        shape = (rows, WIN, D)
        own_grad[:, span, :D] = q_grad.astype(BF16).reshape(shape)
        own_grad[:, span, D : 2 * D] = dot_nn(l_own, q).astype(BF16).reshape(shape)
        own_grad[:, span, 2 * D :] = dot_nn(p_own.astype(BF16), grad).astype(BF16).reshape(shape)
        halo_grad[:, span, :D] = dot_nn(l_halo, q).astype(BF16).reshape(shape)
        halo_grad[:, span, D:] = dot_nn(p_halo.astype(BF16), grad).astype(BF16).reshape(shape)
    for r in range(rows):
        line = slice(r * cols, (r + 1) * cols)
        halo_back[line, :] = dot_nn(back, halo_grad[r]).astype(BF16)
        own_back[line, :] = dot_nn(back, own_grad[r]).astype(BF16)
    halo_term_ref[...] = dot_nt(halo_back[...], project_ref[:, D:]).astype(BF16)
    feature_grad_ref[...] = upstream + dot_nt(own_back[...], project_ref[...])
    own = own_ref[...].reshape(tokens, D)
    halo = halo_ref[...].reshape(tokens, D)
    own_weight = dot_tn(own, own_back[...])
    halo_weight = dot_tn(halo, halo_back[...])
    weight_ref[0] = own_weight[:, :D]
    weight_ref[1] = own_weight[:, D : 2 * D] + halo_weight[:, :D]
    weight_ref[2] = own_weight[:, 2 * D :] + halo_weight[:, D:]


def self_back(
    group, scal, features, halo, qkv, halo_kv, mix, mid_grad, term_low, term_high,
    self_project, self_merge, norm_gains,
):
    rows, cols, _ = halo.shape
    tokens = rows * cols
    return pl.pallas_call(
        functools.partial(self_back_kernel, valid_slot=1 + group),
        grid=(1,),
        in_specs=[
            pl.BlockSpec(memory_space=pltpu.SMEM),
            pl.BlockSpec((rows, cols, D), lambda i: (group, 0, 0)),
            full_spec(halo.shape), full_spec(qkv.shape), full_spec(halo_kv.shape),
            full_spec(mix.shape),
            pl.BlockSpec((tokens, D), lambda i: (group, 0)),
            full_spec(term_low.shape), full_spec(term_high.shape),
            full_spec(self_project.shape), full_spec(self_merge.shape),
            full_spec(norm_gains.shape),
        ],
        out_specs=[
            full_spec((tokens, D)), full_spec((tokens, D)), full_spec((3, D, D)),
            full_spec((D, D)), full_spec((8, D)),
        ],
        out_shape=[
            jax.ShapeDtypeStruct((tokens, D), F32),
            jax.ShapeDtypeStruct((tokens, D), BF16),
            jax.ShapeDtypeStruct((3, D, D), F32),
            jax.ShapeDtypeStruct((D, D), F32),
            jax.ShapeDtypeStruct((8, D), F32),
        ],
        scratch_shapes=[
            pltpu.VMEM((rows, cols, D), BF16),
            pltpu.VMEM((rows, cols, 3 * D), BF16),
            pltpu.VMEM((rows, cols, 2 * D), BF16),
            pltpu.VMEM((tokens, 3 * D), BF16),
            pltpu.VMEM((tokens, 2 * D), BF16),
        ],
        name="self_back",
    )(scal, features, halo, qkv, halo_kv, mix, mid_grad, term_low, term_high,
      self_project, self_merge, norm_gains)


def scattered_sum(pieces, axis):
    count = lax.axis_size(axis)
    place = lax.axis_index(axis)
    current = pieces
    bit = 1
    while bit < count:
        pairs = current.reshape((current.shape[0] // 2, 2) + current.shape[1:])
        odd = (place & bit) != 0
        kept = jnp.where(odd, pairs[:, 1], pairs[:, 0])
        sent = jnp.where(odd, pairs[:, 0], pairs[:, 1]).astype(BF16)
        got = lax.ppermute(sent, axis, [(i, i ^ bit) for i in range(count)])
        current = kept + got.astype(F32)
        bit *= 2
    return current[0]


def body(
    features, window_offsets, self_project, self_merge, cross_project, cross_merge,
    feed_in, feed_out, norm_gains, result_grad,
):
    tile_rows, tile_cols = features.shape[0], features.shape[1]
    half_rows = tile_rows // 2
    tile_tokens = tile_rows * tile_cols
    half_tokens = tile_tokens // 2
    count = lax.axis_size("tiles")
    half_tiles = count // 2
    shift = count // 4
    position = lax.axis_index("tiles")
    image_place = (position + count - shift) % count
    offset = window_offsets[image_place // half_tiles]
    grad_scale = 1.0 / math.sqrt(count * tile_tokens)
    upper_valid = image_place % half_tiles != 0
    lower_valid = image_place % half_tiles != half_tiles - 1
    scal = jnp.stack(
        [offset, upper_valid.astype(jnp.int32), lower_valid.astype(jnp.int32)]
    )
    inner = [
        ((i + shift) % count, (i + 1 + shift) % count)
        for i in range(count)
        if i % half_tiles != half_tiles - 1
    ]
    to_next = inner
    to_previous = [(b, a) for a, b in inner]
    to_partner = [(i, (i + half_tiles) % count) for i in range(count)]

    halos = (
        lax.ppermute(features[half_rows:], "tiles", to_next),
        lax.ppermute(features[:half_rows], "tiles", to_previous),
    )
    parts = [
        self_forward(g, scal, features, halos[g], self_project, self_merge, norm_gains)
        for g in range(2)
    ]
    partners = [lax.ppermute(parts[g][0], "tiles", to_partner) for g in range(2)]
    middles = jnp.concatenate([parts[0][0], parts[1][0]], axis=0)

    block = min(512, half_tokens)
    upstream = result_grad.reshape(tile_tokens, D)
    q, kv_a, open_mix, open_stat = cross_open(block, middles, partners[0], cross_project)
    (kv_b, result, mid_grad, mix_grad, stats, grad_in, grad_out, grad_merge, gain_grad) = (
        cross_close(
            block, middles, partners[1], cross_project, q, open_mix, open_stat,
            cross_merge, feed_in, feed_out, norm_gains, upstream,
        )
    )
    half = half_tokens // 2
    carried, got = None, []
    for c in range(4):
        term, q_grad, cross_weight = cross_back(
            half, c % 2, block, q, mix_grad, stats, (kv_a, kv_b)[c // 2],
            partners[c // 2], cross_project,
            carried=carried, finish=(mid_grad, middles) if c == 3 else None,
        )
        carried = (q_grad, cross_weight)
        got.append(lax.ppermute(term, "tiles", to_partner))
    mid_grad = q_grad
    backs, terms = [], []
    for g in range(2):
        backs.append(
            self_back(
                g, scal, features, halos[g], parts[g][2], parts[g][3], parts[g][1],
                mid_grad, got[2 * g], got[2 * g + 1], self_project, self_merge, norm_gains,
            )
        )
        terms.append(
            lax.ppermute(backs[g][1], "tiles", (to_previous, to_next)[g])
        )
    from_next, from_previous = terms
    features_grad = jnp.concatenate(
        [
            backs[0][0] + from_previous.astype(F32),
            backs[1][0] + from_next.astype(F32),
        ],
        axis=0,
    ).reshape(tile_rows, tile_cols, D)

    self_weight = backs[0][2] + backs[1][2]
    merge_weight = backs[0][3] + backs[1][3]
    gains = jnp.concatenate(
        [backs[0][4][0:1] + backs[1][4][0:1], gain_grad[1:8]], axis=0
    )

    def cut(array):
        return array.reshape(count, array.shape[0] // count, D)

    summed = scattered_sum(
        jnp.concatenate(
            [cut(self_weight[b]) for b in range(3)]
            + [cut(merge_weight)]
            + [cut(cross_weight[b]) for b in range(3)]
            + [cut(grad_merge)]
            + [cut(grad_in[b]) for b in range(grad_in.shape[0])]
            + [cut(grad_out)]
            + [jnp.broadcast_to(gains[None], (count,) + gains.shape)],
            axis=1,
        ),
        "tiles",
    ) * grad_scale
    place = 0

    def take(rows, blocks):
        nonlocal place
        found = [summed[place + b * rows : place + (b + 1) * rows] for b in range(blocks)]
        place += rows * blocks
        return jnp.concatenate(found, axis=1)

    out_self = take(D // count, 3)
    out_self_merge = take(D // count, 1)
    out_cross = take(D // count, 3)
    out_cross_merge = take(D // count, 1)
    out_in = take(2 * D // count, feed_in.shape[1] // D)
    out_out = take(feed_out.shape[0] // count, 1)
    lanes = D // count
    out_gains = lax.dynamic_slice(summed[place : place + 3], (0, position * lanes), (3, lanes))
    return (
        result.reshape(tile_rows, tile_cols, D),
        features_grad,
        out_self,
        out_self_merge,
        out_cross,
        out_cross_merge,
        out_in,
        out_out,
        out_gains,
    )


def solution(mesh):
    whole = P(("groups", "tiles"), None, None)
    rows = P(("groups", "tiles"), None)
    return jax.shard_map(
        body,
        mesh=mesh,
        in_specs=(whole, P("groups"), P(), P(), P(), P(), P(), P(), P(), whole),
        out_specs=(whole, whole, rows, rows, rows, rows, rows, rows, P("groups", "tiles")),
        check_vma=False,
    )
```

profile of v0, /device:TPU:0, one launch (start us, length us, event | category | flops | bytes accessed | tf_op | source)
XLA Modules:
  0.0 153.7 jit_solution(14469498573688802557)
XLA Ops:
  0.6 1.1 fusion.11
  1.7 2.4 %collective-permute-start = (bf16[8,128,128]{2,1,0:T(8,128)(2,1)S(1)}, bf16[8,128,128]{2,1,0:T(8,128)(2,1)S(1)}, u32[]{:S(2)}, u32[]{:S(2)}) collective-permute-start(bf16[8,128,128]{2,1,0:T(8,128)(2,1)S(1)} %get-tuple-element.100), channel_id=1, source_target_pairs={{4,5},{5,6},{6,7},{7,8},{8,9},{9,10},{10,11},{12,13},{13,14},{14,1... | collective-permute-start | bytes 786440 | tf_op jit(solution)/shard_map/ppermute | solution.py:559
  4.1 6.9 %collective-permute-start.1 = (bf16[8,128,128]{2,1,0:T(8,128)(2,1)S(1)}, bf16[8,128,128]{2,1,0:T(8,128)(2,1)S(1)}, u32[]{:S(2)}, u32[]{:S(2)}) collective-permute-start(bf16[8,128,128]{2,1,0:T(8,128)(2,1)S(1)} %get-tuple-element.99), channel_id=1, source_target_pairs={{5,4},{6,5},{7,6},{8,7},{9,8},{10,9},{11,10},{13,12},{14,13},{15,1... | collective-permute-start | bytes 786440 | tf_op jit(solution)/shard_map/ppermute | solution.py:560
  11.1 1.2 dynamic_slice.8
  12.3 1.2 pad_add_fusion.scal_ref
  13.6 0.7 copy-done.3
  14.3 5.0 %self_forward.2 = (bf16[1024,128]{1,0:T(8,128)(2,1)}, bf16[1024,128]{1,0:T(8,128)(2,1)}, bf16[8,128,384]{2,1,0:T(8,128)(2,1)}, bf16[8,128,256]{2,1,0:T(8,128)(2,1)}) custom-call(s32[3]{0:T(128)} %pad_add_fusion.scal_ref, bf16[16,128,128]{2,1,0:T(8,128)(2,1)} %own_ref.7, bf16[8,128,128]{2,1,0:T(8,128)(2,1)} %copy-done.3, bf16[128,384]{1,0:T(8,128)(2,1)} %project_ref.11, ...), custom_call_target="tpu_custom_call" | custom-call | tf_op jit(solution)/shard_map/self_forward/pallas_call | solution.py:125
  19.3 1.2 collective-permute-start.3
  20.5 0.7 copy-done.4
  21.2 5.1 %self_forward.3 = (bf16[1024,128]{1,0:T(8,128)(2,1)}, bf16[1024,128]{1,0:T(8,128)(2,1)}, bf16[8,128,384]{2,1,0:T(8,128)(2,1)}, bf16[8,128,256]{2,1,0:T(8,128)(2,1)}) custom-call(s32[3]{0:T(128)} %pad_add_fusion.scal_ref, bf16[16,128,128]{2,1,0:T(8,128)(2,1)} %own_ref.7, bf16[8,128,128]{2,1,0:T(8,128)(2,1)} %copy-done.4, bf16[128,384]{1,0:T(8,128)(2,1)} %project_ref.11, ...), custom_call_target="tpu_custom_call" | custom-call | tf_op jit(solution)/shard_map/self_forward/pallas_call | solution.py:125
  26.3 1.7 %collective-permute-start.2 = (bf16[1024,128]{1,0:T(8,128)(2,1)}, bf16[1024,128]{1,0:T(8,128)(2,1)S(1)}, u32[]{:S(2)}, u32[]{:S(2)}) collective-permute-start(bf16[1024,128]{1,0:T(8,128)(2,1)} %get-tuple-element.53), channel_id=1, source_target_pairs={{0,8},{1,9},{2,10},{3,11},{4,12},{5,13},{6,14},{7,15},{8,0},{9,1},... | collective-permute-start | bytes 786440 | tf_op jit(solution)/shard_map/ppermute | solution.py:566
  28.0 1.0 constant_dynamic-update-slice_fusion.1
  28.9 1.0 constant_dynamic-update-slice_fusion.middle_ref.refs_9_
  29.9 7.2 %collective-permute-done.3.partner_ref.refs_4_ = bf16[1024,128]{1,0:T(8,128)(2,1)S(1)} collective-permute-done((bf16[1024,128]{1,0:T(8,128)(2,1)}, bf16[1024,128]{1,0:T(8,128)(2,1)S(1)}, u32[]{:S(2)}, u32[]{:S(2)}) %collective-permute-start.3) | collective-permute-done | bytes 262176 | tf_op jit(solution)/shard_map/ppermute | solution.py:566
  37.1 0.7 copy-done.2
  37.8 7.8 %cross_open.1 = (bf16[2048,128]{1,0:T(8,128)(2,1)}, bf16[1024,256]{1,0:T(8,128)(2,1)}, f32[2048,128]{1,0:T(8,128)}, f32[2048,128]{1,0:T(8,128)}) custom-call(bf16[2048,128]{1,0:T(8,128)(2,1)} %copy-done, bf16[1024,128]{1,0:T(8,128)(2,1)} %copy-done.2, bf16[128,384]{1,0:T(8,128)(2,1)} %refs_5_.7), custom_call_target="tpu_custom_call" | custom-call | tf_op jit(solution)/shard_map/cross_open/pallas_call | solution.py:173
  45.6 0.7 copy-done.1
  46.3 18.1 %cross_close.1 = (bf16[1024,256]{1,0:T(8,128)(2,1)}, bf16[2048,128]{1,0:T(8,128)(2,1)}, f32[2048,128]{1,0:T(8,128)}, bf16[2048,128]{1,0:T(8,128)(2,1)}, f32[8,20...) custom-call(bf16[2048,128]{1,0:T(8,128)(2,1)} %copy-done, ...), custom_call_target="tpu_custom_call" | custom-call | tf_op jit(solution)/shard_map/cross_close/pallas_call | solution.py:276
  64.5 6.3 %cross_back.4 = (bf16[512,128]{1,0:T(8,128)(2,1)}, f32[2048,128]{1,0:T(8,128)}, f32[3,128,128]{2,1,0:T(8,128)}) custom-call(bf16[2048,128]{1,0:T(8,128)(2,1)} %get-tuple-element.54.q_ref.refs_0_, bf16[2048,128]{1,0:T(8,128)(2,1)} %get-tuple-element.61.refs_1_, f32[8,2048]{1,0:T(8,128)} %get-tuple-element.62.refs_2_, ...), custom_call_target="tpu_custom_call" | custom-call | tf_op jit(solution)/shard_map/cross_back/pallas_call | solution.py:382
  70.7 6.7 %cross_back.5 = (bf16[512,128]{1,0:T(8,128)(2,1)}, f32[2048,128]{1,0:T(8,128)}, f32[3,128,128]{2,1,0:T(8,128)}) custom-call(bf16[2048,128]{1,0:T(8,128)(2,1)} %get-tuple-element.54.q_ref.refs_0_, bf16[2048,128]{1,0:T(8,128)(2,1)} %get-tuple-element.61.refs_1_, f32[8,2048]{1,0:T(8,128)} %get-tuple-element.62.refs_2_, ...), custom_call_target="tpu_custom_call" | custom-call | tf_op jit(solution)/shard_map/cross_back/pallas_call | solution.py:382
  77.4 6.7 %cross_back.6 = (bf16[512,128]{1,0:T(8,128)(2,1)}, f32[2048,128]{1,0:T(8,128)}, f32[3,128,128]{2,1,0:T(8,128)}) custom-call(bf16[2048,128]{1,0:T(8,128)(2,1)} %get-tuple-element.54.q_ref.refs_0_, bf16[2048,128]{1,0:T(8,128)(2,1)} %get-tuple-element.61.refs_1_, f32[8,2048]{1,0:T(8,128)} %get-tuple-element.62.refs_2_, ...), custom_call_target="tpu_custom_call" | custom-call | tf_op jit(solution)/shard_map/cross_back/pallas_call | solution.py:382
  84.1 7.7 %cross_back.7 = (bf16[512,128]{1,0:T(8,128)(2,1)}, f32[2048,128]{1,0:T(8,128)}, f32[3,128,128]{2,1,0:T(8,128)}) custom-call(bf16[2048,128]{1,0:T(8,128)(2,1)} %get-tuple-element.54.q_ref.refs_0_, bf16[2048,128]{1,0:T(8,128)(2,1)} %get-tuple-element.61.refs_1_, f32[8,2048]{1,0:T(8,128)} %get-tuple-element.62.refs_2_, ...), custom_call_target="tpu_custom_call" | custom-call | tf_op jit(solution)/shard_map/cross_back/pallas_call | solution.py:382
  91.8 2.9 %collective-permute-start.7 = (bf16[512,128]{1,0:T(8,128)(2,1)}, bf16[512,128]{1,0:T(8,128)(2,1)S(1)}, u32[]{:S(2)}, u32[]{:S(2)}) collective-permute-start(bf16[512,128]{1,0:T(8,128)(2,1)} %get-tuple-element.80), channel_id=1, source_target_pairs={{0,8},{1,9},{2,10},{3,11},{4,12},{5,13},{6,14},{7,15},{8,0},{9,1},... | collective-permute-start | bytes 393224 | tf_op jit(solution)/shard_map/ppermute | solution.py:587
  94.8 2.9 %collective-permute-start.5 = (bf16[512,128]{1,0:T(8,128)(2,1)S(1)}, bf16[512,128]{1,0:T(8,128)(2,1)S(1)}, u32[]{:S(2)}, u32[]{:S(2)}) collective-permute-start(bf16[512,128]{1,0:T(8,128)(2,1)S(1)} %copy-done.21), channel_id=1, source_target_pairs={{0,8},{1,9},{2,10},{3,11},{4,12},{5,13},{6,14},{7,15},{8,0},{9,1},... | collective-permute-start | bytes 393224 | tf_op jit(solution)/shard_map/ppermute | solution.py:587
  97.7 0.9 fusion.12
  98.6 8.7 %collective-permute-done.7.term_high_ref = bf16[512,128]{1,0:T(8,128)(2,1)S(1)} collective-permute-done((bf16[512,128]{1,0:T(8,128)(2,1)}, bf16[512,128]{1,0:T(8,128)(2,1)S(1)}, u32[]{:S(2)}, u32[]{:S(2)}) %collective-permute-start.7) | collective-permute-done | bytes 131104 | tf_op jit(solution)/shard_map/ppermute | solution.py:587
  107.3 0.6 copy-done.13
  108.0 7.3 %self_back.3 = (f32[1024,128]{1,0:T(8,128)}, bf16[1024,128]{1,0:T(8,128)(2,1)}, f32[3,128,128]{2,1,0:T(8,128)}, f32[128,128]{1,0:T(8,128)}, f32[8,128]{1,0:T(8,128)}) custom-call(s32[3]{0:T(128)} %pad_add_fusion.scal_ref, bf16[16,128,128]{2,1,0:T(8,128)(2,1)} %own_ref.7, bf16[8,128,128]{2,1,0:T(8,128)(2,1)} %copy-done.4, ...), custom_call_target="tpu_custom_call" | custom-call | tf_op jit(solution)/shard_map/self_back/pallas_call | solution.py:477
  115.3 0.6 copy-done.11
  116.0 7.3 %self_back.2 = (f32[1024,128]{1,0:T(8,128)}, bf16[1024,128]{1,0:T(8,128)(2,1)}, f32[3,128,128]{2,1,0:T(8,128)}, f32[128,128]{1,0:T(8,128)}, f32[8,128]{1,0:T(8,128)}) custom-call(s32[3]{0:T(128)} %pad_add_fusion.scal_ref, bf16[16,128,128]{2,1,0:T(8,128)(2,1)} %own_ref.7, bf16[8,128,128]{2,1,0:T(8,128)(2,1)} %copy-done.3, ...), custom_call_target="tpu_custom_call" | custom-call | tf_op jit(solution)/shard_map/self_back/pallas_call | solution.py:477
  123.3 1.0 add.51
  124.6 0.7 copy-done.8
  125.3 0.7 slice_add_fusion
  126.2 2.2 %collective-permute-start.9 = (bf16[1024,128]{1,0:T(8,128)(2,1)S(1)}, bf16[1024,128]{1,0:T(8,128)(2,1)S(1)}, u32[]{:S(2)}, u32[]{:S(2)}) collective-permute-start(bf16[1024,128]{1,0:T(8,128)(2,1)S(1)} %copy-done.19), channel_id=1, source_target_pairs={{5,4},{6,5},{7,6},{8,7},{9,8},{10,9},{11,10},{13,12},{14,13},{15,1... | collective-permute-start | bytes 786440 | tf_op jit(solution)/shard_map/ppermute | solution.py:598
  128.4 2.3 %collective-permute-start.8 = (bf16[1024,128]{1,0:T(8,128)(2,1)S(1)}, bf16[1024,128]{1,0:T(8,128)(2,1)S(1)}, u32[]{:S(2)}, u32[]{:S(2)}) collective-permute-start(bf16[1024,128]{1,0:T(8,128)(2,1)S(1)} %copy-done.18), channel_id=1, source_target_pairs={{4,5},{5,6},{6,7},{7,8},{8,9},{9,10},{10,11},{12,13},{13,14},{14,1... | collective-permute-start | bytes 786440 | tf_op jit(solution)/shard_map/ppermute | solution.py:598
  130.7 0.1 bitcast_add_fusion
  130.8 1.9 %collective-permute-start.11 = (bf16[4,168,128]{2,1,0:T(8,128)(2,1)S(1)}, bf16[4,168,128]{2,1,0:T(8,128)(2,1)S(1)}, u32[]{:S(2)}, u32[]{:S(2)}) collective-permute-start(bf16[4,168,128]{2,1,0:T(8,128)(2,1)S(1)} %fusion.3), channel_id=1, source_target_pairs={{0,2},{1,3},{2,0},{3,1},{4,6},{5,7},{6,4},{7,5},{8,10},{9,11},{10,... | collective-permute-start | bytes 516104 | tf_op jit(solution)/shard_map/ppermute | solution.py:523
  132.8 7.5 %collective-permute-done.11 = bf16[4,168,128]{2,1,0:T(8,128)(2,1)S(1)} collective-permute-done((bf16[4,168,128]{2,1,0:T(8,128)(2,1)S(1)}, bf16[4,168,128]{2,1,0:T(8,128)(2,1)S(1)}, u32[]{:S(2)}, u32[]{:S(2)}) %collective-permute-start.11) | collective-permute-done | bytes 172064 | tf_op jit(solution)/shard_map/ppermute | solution.py:523
  140.4 0.1 collective-permute-start.12
  140.6 4.8 %collective-permute-done.12 = bf16[2,168,128]{2,1,0:T(8,128)(2,1)S(1)} collective-permute-done((bf16[2,168,128]{2,1,0:T(8,128)(2,1)S(1)}, bf16[2,168,128]{2,1,0:T(8,128)(2,1)S(1)}, u32[]{:S(2)}, u32[]{:S(2)}) %collective-permute-start.12) | collective-permute-done | bytes 86048 | tf_op jit(solution)/shard_map/ppermute | solution.py:523
  145.5 0.2 collective-permute-start.13
  145.6 1.0 pad_maximum_fusion
  146.7 4.0 %collective-permute-done.13 = bf16[1,168,128]{2,1,0:T(8,128)(2,1)S(1)} collective-permute-done((bf16[1,168,128]{2,1,0:T(8,128)(2,1)S(1)}, bf16[1,168,128]{2,1,0:T(8,128)(2,1)S(1)}, u32[]{:S(2)}, u32[]{:S(2)}) %collective-permute-start.13) | collective-permute-done | bytes 43040 | tf_op jit(solution)/shard_map/ppermute | solution.py:523
  150.7 0.6 slice_bitcast_fusion.5
  151.3 0.6 slice_bitcast_fusion
  151.9 0.7 dynamic-slice_bitcast_fusion
  152.5 0.6 pad_maximum_fusion.1
  153.1 0.6 pad_maximum_fusion.2
  (79 shorter events, 0.9 us)
Async XLA Ops:
  1.7 11.8 %collective-permute-start = (bf16[8,128,128]{2,1,0:T(8,128)(2,1)S(1)}, bf16[8,128,128]{2,1,0:T(8,128)(2,1)S(1)}, u32[]{:S(2)}, u32[]{:S(2)}) collective-permute-start(bf16[8,128,128]{2,1,0:T(8,128)(2,1)S(1)} %get-tuple-element.100), channel_id=1, source_target_pairs={{4,5},{5,6},{6,7},{7,8},{8,9},{9,10},{10,11},{12,13},{13,14},{14,1... | collective-permute-start | bytes 786440 | tf_op jit(solution)/shard_map/ppermute | solution.py:559
  4.1 16.4 %collective-permute-start.1 = (bf16[8,128,128]{2,1,0:T(8,128)(2,1)S(1)}, bf16[8,128,128]{2,1,0:T(8,128)(2,1)S(1)}, u32[]{:S(2)}, u32[]{:S(2)}) collective-permute-start(bf16[8,128,128]{2,1,0:T(8,128)(2,1)S(1)} %get-tuple-element.99), channel_id=1, source_target_pairs={{5,4},{6,5},{7,6},{8,7},{9,8},{10,9},{11,10},{13,12},{14,13},{15,1... | collective-permute-start | bytes 786440 | tf_op jit(solution)/shard_map/ppermute | solution.py:560
  13.6 0.7 copy-start.3
  19.3 17.8 %collective-permute-start.3 = (bf16[1024,128]{1,0:T(8,128)(2,1)}, bf16[1024,128]{1,0:T(8,128)(2,1)S(1)}, u32[]{:S(2)}, u32[]{:S(2)}) collective-permute-start(bf16[1024,128]{1,0:T(8,128)(2,1)} %get-tuple-element.52), channel_id=1, source_target_pairs={{0,8},{1,9},{2,10},{3,11},{4,12},{5,13},{6,14},{7,15},{8,0},{9,1},... | collective-permute-start | bytes 786440 | tf_op jit(solution)/shard_map/ppermute | solution.py:566
  20.5 0.7 copy-start.4
  26.3 19.4 %collective-permute-start.2 = (bf16[1024,128]{1,0:T(8,128)(2,1)}, bf16[1024,128]{1,0:T(8,128)(2,1)S(1)}, u32[]{:S(2)}, u32[]{:S(2)}) collective-permute-start(bf16[1024,128]{1,0:T(8,128)(2,1)} %get-tuple-element.53), channel_id=1, source_target_pairs={{0,8},{1,9},{2,10},{3,11},{4,12},{5,13},{6,14},{7,15},{8,0},{9,1},... | collective-permute-start | bytes 786440 | tf_op jit(solution)/shard_map/ppermute | solution.py:566
  29.9 7.2 %copy-start = (bf16[2048,128]{1,0:T(8,128)(2,1)}, bf16[2048,128]{1,0:T(8,128)(2,1)S(1)}, u32[]{:S(2)}) copy-start(bf16[2048,128]{1,0:T(8,128)(2,1)S(1)} %constant_dynamic-update-slice_fusion.middle_ref.refs_9_) | copy-start | bytes 1572868
  37.1 0.7 copy-start.2
  45.6 0.7 copy-start.1
  84.1 14.5 %collective-permute-start.6 = (bf16[512,128]{1,0:T(8,128)(2,1)}, bf16[512,128]{1,0:T(8,128)(2,1)S(1)}, u32[]{:S(2)}, u32[]{:S(2)}) collective-permute-start(bf16[512,128]{1,0:T(8,128)(2,1)} %get-tuple-element.79), channel_id=1, source_target_pairs={{0,8},{1,9},{2,10},{3,11},{4,12},{5,13},{6,14},{7,15},{8,0},{9,1},... | collective-permute-start | bytes 393224 | tf_op jit(solution)/shard_map/ppermute | solution.py:587
  84.1 10.6 %copy-start.20 = (bf16[512,128]{1,0:T(8,128)(2,1)S(1)}, bf16[512,128]{1,0:T(8,128)(2,1)}, u32[]{:S(2)}) copy-start(bf16[512,128]{1,0:T(8,128)(2,1)} %get-tuple-element.73) | copy-start | bytes 393220
  84.1 10.7 %copy-start.21 = (bf16[512,128]{1,0:T(8,128)(2,1)S(1)}, bf16[512,128]{1,0:T(8,128)(2,1)}, u32[]{:S(2)}) copy-start(bf16[512,128]{1,0:T(8,128)(2,1)} %get-tuple-element.74) | copy-start | bytes 393220
  84.1 13.5 %copy-start.7 = (f32[4,256,128]{2,1,0:T(8,128)S(1)}, f32[4,256,128]{2,1,0:T(8,128)}, u32[]{:S(2)}) copy-start(f32[4,256,128]{2,1,0:T(8,128)} %get-tuple-element.90) | copy-start | bytes 1572868
  84.1 13.6 %copy-start.17 = (f32[8,128]{1,0:T(8,128)S(1)}, f32[8,128]{1,0:T(8,128)}, u32[]{:S(2)}) copy-start(f32[8,128]{1,0:T(8,128)} %get-tuple-element.94) | copy-start | bytes 12292
  91.8 15.5 %collective-permute-start.7 = (bf16[512,128]{1,0:T(8,128)(2,1)}, bf16[512,128]{1,0:T(8,128)(2,1)S(1)}, u32[]{:S(2)}, u32[]{:S(2)}) collective-permute-start(bf16[512,128]{1,0:T(8,128)(2,1)} %get-tuple-element.80), channel_id=1, source_target_pairs={{0,8},{1,9},{2,10},{3,11},{4,12},{5,13},{6,14},{7,15},{8,0},{9,1},... | collective-permute-start | bytes 393224 | tf_op jit(solution)/shard_map/ppermute | solution.py:587
  94.7 20.6 %collective-permute-start.4 = (bf16[512,128]{1,0:T(8,128)(2,1)S(1)}, bf16[512,128]{1,0:T(8,128)(2,1)S(1)}, u32[]{:S(2)}, u32[]{:S(2)}) collective-permute-start(bf16[512,128]{1,0:T(8,128)(2,1)S(1)} %copy-done.20), channel_id=1, source_target_pairs={{0,8},{1,9},{2,10},{3,11},{4,12},{5,13},{6,14},{7,15},{8,0},{9,1},... | collective-permute-start | bytes 393224 | tf_op jit(solution)/shard_map/ppermute | solution.py:587
  94.8 20.5 %collective-permute-start.5 = (bf16[512,128]{1,0:T(8,128)(2,1)S(1)}, bf16[512,128]{1,0:T(8,128)(2,1)S(1)}, u32[]{:S(2)}, u32[]{:S(2)}) collective-permute-start(bf16[512,128]{1,0:T(8,128)(2,1)S(1)} %copy-done.21), channel_id=1, source_target_pairs={{0,8},{1,9},{2,10},{3,11},{4,12},{5,13},{6,14},{7,15},{8,0},{9,1},... | collective-permute-start | bytes 393224 | tf_op jit(solution)/shard_map/ppermute | solution.py:587
  98.6 8.7 %copy-start.10 = (bf16[512,128]{1,0:T(8,128)(2,1)}, bf16[512,128]{1,0:T(8,128)(2,1)S(1)}, u32[]{:S(2)}) copy-start(bf16[512,128]{1,0:T(8,128)(2,1)S(1)} %collective-permute-done.6.term_low_ref) | copy-start | bytes 393220
  107.3 0.7 copy-start.13
  115.3 0.6 copy-start.11
  115.3 0.7 copy-start.12
  116.0 7.3 %copy-start.9 = (f32[3,128,128]{2,1,0:T(8,128)S(1)}, f32[3,128,128]{2,1,0:T(8,128)}, u32[]{:S(2)}) copy-start(f32[3,128,128]{2,1,0:T(8,128)} %get-tuple-element.85) | copy-start | bytes 589828
  123.3 1.1 copy-start.14
  123.3 1.1 copy-start.15
  123.3 1.2 copy-start.16
  124.3 1.0 copy-start.8
  124.5 1.7 %copy-start.19 = (bf16[1024,128]{1,0:T(8,128)(2,1)S(1)}, bf16[1024,128]{1,0:T(8,128)(2,1)}, u32[]{:S(2)}) copy-start(bf16[1024,128]{1,0:T(8,128)(2,1)} %get-tuple-element.83) | copy-start | bytes 786436
  124.5 3.9 %copy-start.18 = (bf16[1024,128]{1,0:T(8,128)(2,1)S(1)}, bf16[1024,128]{1,0:T(8,128)(2,1)}, u32[]{:S(2)}) copy-start(bf16[1024,128]{1,0:T(8,128)(2,1)} %get-tuple-element.81) | copy-start | bytes 786436
  126.1 4.6 %collective-permute-start.10 = (bf16[8,168,128]{2,1,0:T(8,128)(2,1)S(1)}, bf16[8,168,128]{2,1,0:T(8,128)(2,1)S(1)}, u32[]{:S(2)}, u32[]{:S(2)}) collective-permute-start(bf16[8,168,128]{2,1,0:T(8,128)(2,1)S(1)} %fusion), channel_id=1, source_target_pairs={{0,1},{1,0},{2,3},{3,2},{4,5},{5,4},{6,7},{7,6},{8,9},{9,8},{10,11... | collective-permute-start | bytes 1032200 | tf_op jit(solution)/shard_map/ppermute | solution.py:523
  126.2 6.6 %collective-permute-start.9 = (bf16[1024,128]{1,0:T(8,128)(2,1)S(1)}, bf16[1024,128]{1,0:T(8,128)(2,1)S(1)}, u32[]{:S(2)}, u32[]{:S(2)}) collective-permute-start(bf16[1024,128]{1,0:T(8,128)(2,1)S(1)} %copy-done.19), channel_id=1, source_target_pairs={{5,4},{6,5},{7,6},{8,7},{9,8},{10,9},{11,10},{13,12},{14,13},{15,1... | collective-permute-start | bytes 786440 | tf_op jit(solution)/shard_map/ppermute | solution.py:598
  128.4 4.4 %copy-start.5 = (f32[1024,128]{1,0:T(8,128)S(1)}, f32[1024,128]{1,0:T(8,128)}, u32[]{:S(2)}) copy-start(f32[1024,128]{1,0:T(8,128)} %get-tuple-element.82) | copy-start | bytes 1572868
  128.4 12.1 %collective-permute-start.8 = (bf16[1024,128]{1,0:T(8,128)(2,1)S(1)}, bf16[1024,128]{1,0:T(8,128)(2,1)S(1)}, u32[]{:S(2)}, u32[]{:S(2)}) collective-permute-start(bf16[1024,128]{1,0:T(8,128)(2,1)S(1)} %copy-done.18), channel_id=1, source_target_pairs={{4,5},{5,6},{6,7},{7,8},{8,9},{9,10},{10,11},{12,13},{13,14},{14,1... | collective-permute-start | bytes 786440 | tf_op jit(solution)/shard_map/ppermute | solution.py:598
  130.8 9.5 %collective-permute-start.11 = (bf16[4,168,128]{2,1,0:T(8,128)(2,1)S(1)}, bf16[4,168,128]{2,1,0:T(8,128)(2,1)S(1)}, u32[]{:S(2)}, u32[]{:S(2)}) collective-permute-start(bf16[4,168,128]{2,1,0:T(8,128)(2,1)S(1)} %fusion.3), channel_id=1, source_target_pairs={{0,2},{1,3},{2,0},{3,1},{4,6},{5,7},{6,4},{7,5},{8,10},{9,11},{10,... | collective-permute-start | bytes 516104 | tf_op jit(solution)/shard_map/ppermute | solution.py:523
  132.8 7.7 %copy-start.6 = (f32[1024,128]{1,0:T(8,128)S(1)}, f32[1024,128]{1,0:T(8,128)}, u32[]{:S(2)}) copy-start(f32[1024,128]{1,0:T(8,128)} %get-tuple-element.75) | copy-start | bytes 1572868
  140.4 5.0 %collective-permute-start.12 = (bf16[2,168,128]{2,1,0:T(8,128)(2,1)S(1)}, bf16[2,168,128]{2,1,0:T(8,128)(2,1)S(1)}, u32[]{:S(2)}, u32[]{:S(2)}) collective-permute-start(bf16[2,168,128]{2,1,0:T(8,128)(2,1)S(1)} %fusion.7), channel_id=1, source_target_pairs={{0,4},{1,5},{2,6},{3,7},{4,0},{5,1},{6,2},{7,3},{8,12},{9,13},{10,... | collective-permute-start | bytes 258056 | tf_op jit(solution)/shard_map/ppermute | solution.py:523
  145.5 5.2 %collective-permute-start.13 = (bf16[1,168,128]{2,1,0:T(8,128)(2,1)S(1)}, bf16[1,168,128]{2,1,0:T(8,128)(2,1)S(1)}, u32[]{:S(2)}, u32[]{:S(2)}) collective-permute-start(bf16[1,168,128]{2,1,0:T(8,128)(2,1)S(1)} %fusion.9), channel_id=1, source_target_pairs={{0,8},{1,9},{2,10},{3,11},{4,12},{5,13},{6,14},{7,15},{8,0},{9,1},... | collective-permute-start | bytes 129032 | tf_op jit(solution)/shard_map/ppermute | solution.py:523
where the time goes:
time: 154 us
  Pallas kernels  77.8 us (51%)
  waiting for transfers between devices  32.2 us (21%)
  starting transfers between devices  24.8 us (16%)
  local copies, waits for them, and re-layouts  12.1 us (8%)
  other arithmetic  5.65 us (4%)
    pallas_call x4, Pallas kernels, cross_back(): pl.pallas_call(functools.partial(cross_back_kernel, first=first, last=las...  27.3 us
    pallas_call x1, Pallas kernels, cross_close(): pl.pallas_call(cross_close_kernel, grid=(tokens // block,), in_specs=[til...  18.1 us
    ppermute x4, waiting for transfers between devices, scattered_sum(): got = lax.ppermute(sent, axis, [(i, i ^ bit) for i in range(count)])  16.3 us
    pallas_call x2, Pallas kernels, self_back(): pl.pallas_call(functools.partial(self_back_kernel, valid_slot=1 + group),...  14.6 us
    pallas_call x2, Pallas kernels, self_forward(): pl.pallas_call(functools.partial(self_forward_kernel, valid_slot=1 + grou...  10.1 us
    ppermute x4, waiting for transfers between devices, body(): got.append(lax.ppermute(term, 'tiles', to_partner))  8.72 us
    pallas_call x1, Pallas kernels, cross_open(): pl.pallas_call(cross_open_kernel, grid=(tokens // block,), in_specs=[pl.B...  7.79 us
    ppermute x2, waiting for transfers between devices, body(): lax.ppermute(parts[g][0], 'tiles', to_partner)  7.19 us
  transfers between devices with their start and end apart: 14, of which 5 were waited for; matrix products, arithmetic and copies ran while one was open for 4% of the time, Pallas kernels for 21%

commit v1 on v0

--- a/solution.py
+++ b/solution.py
@@ -20,8 +20,18 @@
 SCALE = D ** (-0.5)
 
 
+LOCAL_LIMIT = pltpu.CompilerParams(vmem_limit_bytes=20 * 2**20)
+
 F32 = jnp.float32
 BF16 = jnp.bfloat16
+
+
+def on_chip(array):
+    return pltpu.with_memory_space_constraint(array, pltpu.VMEM)
+
+
+def off_chip(array):
+    return pltpu.with_memory_space_constraint(array, pltpu.HBM)
 
 
 def dot_nn(a, b):
@@ -141,11 +151,12 @@
         ],
         out_shape=[
             jax.ShapeDtypeStruct((tokens, D), BF16),
-            jax.ShapeDtypeStruct((tokens, D), BF16),
-            jax.ShapeDtypeStruct((rows, cols, 3 * D), BF16),
-            jax.ShapeDtypeStruct((rows, cols, 2 * D), BF16),
+            pltpu.VMEM((tokens, D), BF16),
+            pltpu.VMEM((rows, cols, 3 * D), BF16),
+            pltpu.VMEM((rows, cols, 2 * D), BF16),
         ],
         scratch_shapes=[pltpu.VMEM((rows, cols, D), BF16)] * 3,
+        compiler_params=LOCAL_LIMIT,
         name="self_forward",
     )(scal, features, halo, self_project, self_merge, norm_gains)
 
@@ -190,6 +201,7 @@
             jax.ShapeDtypeStruct((tokens, D), F32),
             jax.ShapeDtypeStruct((tokens, D), F32),
         ],
+        compiler_params=LOCAL_LIMIT,
         name="cross_open",
     )(middles, partner, cross_project)
 
@@ -298,6 +310,7 @@
             jax.ShapeDtypeStruct((D, D), F32),
             jax.ShapeDtypeStruct((8, D), F32),
         ],
+        compiler_params=LOCAL_LIMIT,
         name="cross_close",
     )(middles, partner, cross_project, q, open_mix, open_stat,
       cross_merge, feed_in, feed_out, norm_gains, upstream)
@@ -394,6 +407,7 @@
         scratch_shapes=[
             pltpu.VMEM((block, D), F32), pltpu.VMEM((block, D), F32), pltpu.VMEM((tokens, D), F32)
         ],
+        compiler_params=LOCAL_LIMIT,
         name="cross_back",
     )(*args)
 
@@ -505,6 +519,7 @@
             pltpu.VMEM((tokens, 3 * D), BF16),
             pltpu.VMEM((tokens, 2 * D), BF16),
         ],
+        compiler_params=LOCAL_LIMIT,
         name="self_back",
     )(scal, features, halo, qkv, halo_kv, mix, mid_grad, term_low, term_high,
       self_project, self_merge, norm_gains)
@@ -555,9 +570,17 @@
     to_previous = [(b, a) for a, b in inner]
     to_partner = [(i, (i + half_tiles) % count) for i in range(count)]
 
+    raw_features = features
+    features = off_chip(features)
+    self_project, self_merge, cross_project, cross_merge, feed_in, feed_out, norm_gains = (
+        off_chip(w)
+        for w in (
+            self_project, self_merge, cross_project, cross_merge, feed_in, feed_out, norm_gains
+        )
+    )
     halos = (
-        lax.ppermute(features[half_rows:], "tiles", to_next),
-        lax.ppermute(features[:half_rows], "tiles", to_previous),
+        lax.ppermute(raw_features[half_rows:], "tiles", to_next),
+        lax.ppermute(raw_features[:half_rows], "tiles", to_previous),
     )
     parts = [
         self_forward(g, scal, features, halos[g], self_project, self_merge, norm_gains)
@@ -567,7 +590,7 @@
     middles = jnp.concatenate([parts[0][0], parts[1][0]], axis=0)
 
     block = min(512, half_tokens)
-    upstream = result_grad.reshape(tile_tokens, D)
+    upstream = off_chip(result_grad.reshape(tile_tokens, D))
     q, kv_a, open_mix, open_stat = cross_open(block, middles, partners[0], cross_project)
     (kv_b, result, mid_grad, mix_grad, stats, grad_in, grad_out, grad_merge, gain_grad) = (
         cross_close(
@@ -590,7 +613,8 @@
     for g in range(2):
         backs.append(
             self_back(
-                g, scal, features, halos[g], parts[g][2], parts[g][3], parts[g][1],
+                g, scal, features, halos[g],
+                on_chip(parts[g][2]), on_chip(parts[g][3]), on_chip(parts[g][1]),
                 mid_grad, got[2 * g], got[2 * g + 1], self_project, self_merge, norm_gains,
             )
         )

time: 154 us -> 149 us (0.968)
  Pallas kernels: 77.8 us -> 65.5 us
  local copies, waits for them, and re-layouts: 12.1 us -> 17.6 us
    pallas_call x4, Pallas kernels: 27.3 us -> 19.6 us  [cross_back(): pl.pallas_call(functools.partial(cross_back_kernel, first=first, last=las...]
    unnamed x58 -> x26, local copies, waits for them, and re-layouts: 5.94 us -> 11.8 us
    pallas_call x2, Pallas kernels: 14.6 us -> 11.7 us  [self_back(): pl.pallas_call(functools.partial(self_back_kernel, valid_slot=1 + group),...]
    ppermute x2, starting transfers between devices: 4.46 us -> 6.56 us  [body(): terms.append(lax.ppermute(backs[g][1], 'tiles', (to_previous, to_next)[g]))]
  transfers between devices with their start and end apart: 14 -> 14, of which waited for: 5 -> 6; matrix products, arithmetic and copies ran while one was open for 4% -> 4% of each run, Pallas kernels for 21% -> 19%
where the time goes in v1:
time: 149 us; the launch traced here: 148 us
  Pallas kernels  65.5 us (44%)
  waiting for transfers between devices  32.8 us (22%)
  starting transfers between devices  25.5 us (17%)
  local copies, waits for them, and re-layouts  17.6 us (12%)
  other arithmetic  6.05 us (4%)
    pallas_call x4, Pallas kernels, cross_back(): pl.pallas_call(functools.partial(cross_back_kernel, first=first, last=las...  19.6 us
    pallas_call x1, Pallas kernels, cross_close(): pl.pallas_call(cross_close_kernel, grid=(tokens // block,), in_specs=[til...  17.5 us
    ppermute x4, waiting for transfers between devices, scattered_sum(): got = lax.ppermute(sent, axis, [(i, i ^ bit) for i in range(count)])  16.9 us
    unnamed x26, local copies, waits for them, and re-layouts  11.8 us
    pallas_call x2, Pallas kernels, self_back(): pl.pallas_call(functools.partial(self_back_kernel, valid_slot=1 + group),...  11.7 us
    pallas_call x2, Pallas kernels, self_forward(): pl.pallas_call(functools.partial(self_forward_kernel, valid_slot=1 + grou...  9.86 us
    ppermute x4, waiting for transfers between devices, body(): got.append(lax.ppermute(term, 'tiles', to_partner))  9.38 us
    ppermute x1, starting transfers between devices, body(): lax.ppermute(raw_features[:half_rows], 'tiles', to_previous)  6.9 us
  transfers between devices with their start and end apart: 14, of which 6 were waited for; matrix products, arithmetic and copies ran while one was open for 4% of the time, Pallas kernels for 19%

profile of v1, /device:TPU:0, one launch (start us, length us, event | category | flops | bytes accessed | tf_op | source)
XLA Modules:
  0.0 148.5 jit_solution(17751731100330761620)
XLA Ops:
  0.6 1.1 fusion.11
  1.7 2.4 %collective-permute-start = (bf16[8,128,128]{2,1,0:T(8,128)(2,1)S(1)}, bf16[8,128,128]{2,1,0:T(8,128)(2,1)S(1)}, u32[]{:S(2)}, u32[]{:S(2)}) collective-permute-start(bf16[8,128,128]{2,1,0:T(8,128)(2,1)S(1)} %get-tuple-element.100), channel_id=1, source_target_pairs={{4,5},{5,6},{6,7},{7,8},{8,9},{9,10},{10,11},{12,13},{13,14},{14,1... | collective-permute-start | bytes 786440 | tf_op jit(solution)/shard_map/ppermute | solution.py:582
  4.1 6.9 %collective-permute-start.1 = (bf16[8,128,128]{2,1,0:T(8,128)(2,1)S(1)}, bf16[8,128,128]{2,1,0:T(8,128)(2,1)S(1)}, u32[]{:S(2)}, u32[]{:S(2)}) collective-permute-start(bf16[8,128,128]{2,1,0:T(8,128)(2,1)S(1)} %get-tuple-element.99), channel_id=1, source_target_pairs={{5,4},{6,5},{7,6},{8,7},{9,8},{10,9},{11,10},{13,12},{14,13},{15,1... | collective-permute-start | bytes 786440 | tf_op jit(solution)/shard_map/ppermute | solution.py:583
  11.1 1.2 dynamic_slice.8
  12.3 0.7 pad_add_fusion.scal_ref
  13.2 4.9 %self_forward.2 = (bf16[1024,128]{1,0:T(8,128)(2,1)}, bf16[1024,128]{1,0:T(8,128)(2,1)S(1)}, bf16[8,128,384]{2,1,0:T(8,128)(2,1)S(1)}, bf16[8,128,256]{2,1,0:T(8,128)(2,1)S(1)}) custom-call(s32[3]{0:T(128)S(1)} %pad_add_fusion.scal_ref, bf16[16,128,128]{2,1,0:T(8,128)(2,1)} %own_ref.7, bf16[8,128,128]{2,1,0:T(8,128)(2,1)S(1)} %collective-permute-done.halo_ref, ...), custom_call_target="tpu_custom_call" | custom-call | tf_op jit(solution)/shard_map/self_forward/pallas_call | solution.py:135
  18.2 1.1 collective-permute-start.3
  19.3 4.9 %self_forward.3 = (bf16[1024,128]{1,0:T(8,128)(2,1)}, bf16[1024,128]{1,0:T(8,128)(2,1)S(1)}, bf16[8,128,384]{2,1,0:T(8,128)(2,1)S(1)}, bf16[8,128,256]{2,1,0:T(8,128)(2,1)S(1)}) custom-call(s32[3]{0:T(128)S(1)} %pad_add_fusion.scal_ref, bf16[16,128,128]{2,1,0:T(8,128)(2,1)} %own_ref.7, bf16[8,128,128]{2,1,0:T(8,128)(2,1)S(1)} %collective-permute-done.1.halo_ref, ...), custom_call_target="tpu_custom_call" | custom-call | tf_op jit(solution)/shard_map/self_forward/pallas_call | solution.py:135
  24.2 0.8 copy-done
  25.0 0.7 copy-done.2
  25.7 1.8 %collective-permute-start.2 = (bf16[1024,128]{1,0:T(8,128)(2,1)}, bf16[1024,128]{1,0:T(8,128)(2,1)S(1)}, u32[]{:S(2)}, u32[]{:S(2)}) collective-permute-start(bf16[1024,128]{1,0:T(8,128)(2,1)} %get-tuple-element.53), channel_id=1, source_target_pairs={{0,8},{1,9},{2,10},{3,11},{4,12},{5,13},{6,14},{7,15},{8,0},{9,1},... | collective-permute-start | bytes 786440 | tf_op jit(solution)/shard_map/ppermute | solution.py:589
  27.5 1.0 constant_dynamic-update-slice_fusion.1
  28.5 1.0 constant_dynamic-update-slice_fusion.middle_ref.refs_9_
  29.5 6.3 %collective-permute-done.3.partner_ref.refs_4_ = bf16[1024,128]{1,0:T(8,128)(2,1)S(1)} collective-permute-done((bf16[1024,128]{1,0:T(8,128)(2,1)}, bf16[1024,128]{1,0:T(8,128)(2,1)S(1)}, u32[]{:S(2)}, u32[]{:S(2)}) %collective-permute-start.3) | collective-permute-done | bytes 262176 | tf_op jit(solution)/shard_map/ppermute | solution.py:589
  35.8 6.8 %cross_open.1 = (bf16[2048,128]{1,0:T(8,128)(2,1)S(1)}, bf16[1024,256]{1,0:T(8,128)(2,1)S(1)}, f32[2048,128]{1,0:T(8,128)S(1)}, f32[2048,128]{1,0:T(8,128)S(1)}) custom-call(bf16[2048,128]{1,0:T(8,128)(2,1)S(1)} %constant_dynamic-update-slice_fusion.middle_ref.refs_9_, bf16[1024,128]{1,0:T(8,128)(2,1)S(1)} %collective-permute-done.3.partner_ref.refs_4_, ...), custom_call_target="tpu_custom_call" | custom-call | tf_op jit(solution)/shard_map/cross_open/pallas_call | solution.py:184
  42.7 17.5 %cross_close.1 = (bf16[1024,256]{1,0:T(8,128)(2,1)S(1)}, bf16[2048,128]{1,0:T(8,128)(2,1)}, f32[2048,128]{1,0:T(8,128)S(1)}, bf16[2048,128]{1,0:T(8,128)(2,1)S(1...) custom-call(bf16[2048,128]{1,0:T(8,128)(2,1)S(1)} %constant_dynamic-, ...), custom_call_target="tpu_custom_call" | custom-call | tf_op jit(solution)/shard_map/cross_close/pallas_call | solution.py:288
  60.2 4.8 %cross_back.4 = (bf16[512,128]{1,0:T(8,128)(2,1)S(1)}, f32[2048,128]{1,0:T(8,128)S(1)}, f32[3,128,128]{2,1,0:T(8,128)S(1)}) custom-call(bf16[2048,128]{1,0:T(8,128)(2,1)S(1)} %get-tuple-element.54.q_ref.refs_0_, bf16[2048,128]{1,0:T(8,128)(2,1)S(1)} %get-tuple-element.61.refs_1_, f32[8,2048]{1,0:T(8,128)S(1)} %get-tuple-element.62.refs_2_, ...), custom_call_target="tpu_custom_call" | custom-call | tf_op jit(solution)/shard_map/cross_back/pallas_call | solution.py:395
  64.9 4.8 %cross_back.5 = (bf16[512,128]{1,0:T(8,128)(2,1)S(1)}, f32[2048,128]{1,0:T(8,128)S(1)}, f32[3,128,128]{2,1,0:T(8,128)S(1)}) custom-call(bf16[2048,128]{1,0:T(8,128)(2,1)S(1)} %get-tuple-element.54.q_ref.refs_0_, bf16[2048,128]{1,0:T(8,128)(2,1)S(1)} %get-tuple-element.61.refs_1_, f32[8,2048]{1,0:T(8,128)S(1)} %get-tuple-element.62.refs_2_, ...), custom_call_target="tpu_custom_call" | custom-call | tf_op jit(solution)/shard_map/cross_back/pallas_call | solution.py:395
  69.7 4.8 %cross_back.6 = (bf16[512,128]{1,0:T(8,128)(2,1)S(1)}, f32[2048,128]{1,0:T(8,128)S(1)}, f32[3,128,128]{2,1,0:T(8,128)S(1)}) custom-call(bf16[2048,128]{1,0:T(8,128)(2,1)S(1)} %get-tuple-element.54.q_ref.refs_0_, bf16[2048,128]{1,0:T(8,128)(2,1)S(1)} %get-tuple-element.61.refs_1_, f32[8,2048]{1,0:T(8,128)S(1)} %get-tuple-element.62.refs_2_, ...), custom_call_target="tpu_custom_call" | custom-call | tf_op jit(solution)/shard_map/cross_back/pallas_call | solution.py:395
  74.6 5.3 %cross_back.7 = (bf16[512,128]{1,0:T(8,128)(2,1)S(1)}, f32[2048,128]{1,0:T(8,128)S(1)}, f32[3,128,128]{2,1,0:T(8,128)S(1)}) custom-call(bf16[2048,128]{1,0:T(8,128)(2,1)S(1)} %get-tuple-element.54.q_ref.refs_0_, bf16[2048,128]{1,0:T(8,128)(2,1)S(1)} %get-tuple-element.61.refs_1_, f32[8,2048]{1,0:T(8,128)S(1)} %get-tuple-element.62.refs_2_, ...), custom_call_target="tpu_custom_call" | custom-call | tf_op jit(solution)/shard_map/cross_back/pallas_call | solution.py:395
  79.9 3.0 %collective-permute-start.7 = (bf16[512,128]{1,0:T(8,128)(2,1)S(1)}, bf16[512,128]{1,0:T(8,128)(2,1)S(1)}, u32[]{:S(2)}, u32[]{:S(2)}) collective-permute-start(bf16[512,128]{1,0:T(8,128)(2,1)S(1)} %get-tuple-element.80), channel_id=1, source_target_pairs={{0,8},{1,9},{2,10},{3,11},{4,12},{5,13},{6,14},{7,15},{8,0},{9,1},... | collective-permute-start | bytes 393224 | tf_op jit(solution)/shard_map/ppermute | solution.py:610
  82.9 2.8 %collective-permute-start.5 = (bf16[512,128]{1,0:T(8,128)(2,1)S(1)}, bf16[512,128]{1,0:T(8,128)(2,1)S(1)}, u32[]{:S(2)}, u32[]{:S(2)}) collective-permute-start(bf16[512,128]{1,0:T(8,128)(2,1)S(1)} %get-tuple-element.74), channel_id=1, source_target_pairs={{0,8},{1,9},{2,10},{3,11},{4,12},{5,13},{6,14},{7,15},{8,0},{9,1},... | collective-permute-start | bytes 393224 | tf_op jit(solution)/shard_map/ppermute | solution.py:610
  85.9 9.4 %collective-permute-done.7.term_high_ref = bf16[512,128]{1,0:T(8,128)(2,1)S(1)} collective-permute-done((bf16[512,128]{1,0:T(8,128)(2,1)S(1)}, bf16[512,128]{1,0:T(8,128)(2,1)S(1)}, u32[]{:S(2)}, u32[]{:S(2)}) %collective-permute-start.7) | collective-permute-done | bytes 131104 | tf_op jit(solution)/shard_map/ppermute | solution.py:610
  95.3 5.8 %self_back.3 = (f32[1024,128]{1,0:T(8,128)S(1)}, bf16[1024,128]{1,0:T(8,128)(2,1)S(1)}, f32[3,128,128]{2,1,0:T(8,128)S(1)}, f32[128,128]{1,0:T(8,128)S(1)}, f32[8,128]{1,0:T(8,128)S(1)}) custom-call(s32[3]{0:T(128)S(1)} %pad_add_fusion.scal_ref, bf16[16,128,128]{2,1,0:T(8,128)(2,1)} %own_ref.7, bf16[8,128,128]{2,1,0:T(8,128)(2,1)S(1)} %collective-permute-done.1.halo_ref, ...), custom_call_target="tpu_custom_call" | custom-call | tf_op jit(solution)/shard_map/self_back/pallas_call | solution.py:491
  101.1 0.7 copy-done.4
  101.8 5.8 %self_back.2 = (f32[1024,128]{1,0:T(8,128)S(1)}, bf16[1024,128]{1,0:T(8,128)(2,1)S(1)}, f32[3,128,128]{2,1,0:T(8,128)S(1)}, f32[128,128]{1,0:T(8,128)S(1)}, f32[8,128]{1,0:T(8,128)S(1)}) custom-call(s32[3]{0:T(128)S(1)} %pad_add_fusion.scal_ref, bf16[16,128,128]{2,1,0:T(8,128)(2,1)} %own_ref.7, bf16[8,128,128]{2,1,0:T(8,128)(2,1)S(1)} %collective-permute-done.halo_ref, ...), custom_call_target="tpu_custom_call" | custom-call | tf_op jit(solution)/shard_map/self_back/pallas_call | solution.py:491
  107.7 0.6 copy_dynamic-update-slice_fusion.12
  108.3 0.7 copy_dynamic-update-slice_fusion.11
  109.0 0.6 copy_dynamic-update-slice_fusion.10
  109.6 0.7 copy_dynamic-update-slice_fusion.9
  110.3 0.6 copy_dynamic-update-slice_fusion.8
  110.9 0.6 copy_dynamic-update-slice_fusion.7
  111.6 0.7 copy_dynamic-update-slice_fusion.6
  112.8 0.7 copy_dynamic-update-slice_fusion.4
  113.5 0.7 copy_dynamic-update-slice_fusion.3
  114.2 0.7 copy_dynamic-update-slice_fusion.2
  114.9 0.7 copy_dynamic-update-slice_fusion.1
  115.5 0.8 copy_dynamic-update-slice_fusion
  116.3 0.6 constant_dynamic-update-slice_fusion.2
  117.0 1.4 fusion
  118.4 4.6 %collective-permute-start.9 = (bf16[1024,128]{1,0:T(8,128)(2,1)S(1)}, bf16[1024,128]{1,0:T(8,128)(2,1)S(1)}, u32[]{:S(2)}, u32[]{:S(2)}) collective-permute-start(bf16[1024,128]{1,0:T(8,128)(2,1)S(1)} %get-tuple-element.83), channel_id=1, source_target_pairs={{5,4},{6,5},{7,6},{8,7},{9,8},{10,9},{11,10},{13,12},{14,13},{15,1... | collective-permute-start | bytes 786440 | tf_op jit(solution)/shard_map/ppermute | solution.py:622
  123.1 1.9 %collective-permute-start.8 = (bf16[1024,128]{1,0:T(8,128)(2,1)S(1)}, bf16[1024,128]{1,0:T(8,128)(2,1)S(1)}, u32[]{:S(2)}, u32[]{:S(2)}) collective-permute-start(bf16[1024,128]{1,0:T(8,128)(2,1)S(1)} %copy-done.5), channel_id=1, source_target_pairs={{4,5},{5,6},{6,7},{7,8},{8,9},{9,10},{10,11},{12,13},{13,14},{14,1... | collective-permute-start | bytes 786440 | tf_op jit(solution)/shard_map/ppermute | solution.py:622
  125.0 1.4 bitcast_add_fusion
  127.1 8.6 %collective-permute-done.11 = bf16[4,168,128]{2,1,0:T(8,128)(2,1)S(1)} collective-permute-done((bf16[4,168,128]{2,1,0:T(8,128)(2,1)S(1)}, bf16[4,168,128]{2,1,0:T(8,128)(2,1)S(1)}, u32[]{:S(2)}, u32[]{:S(2)}) %collective-permute-start.11) | collective-permute-done | bytes 172064 | tf_op jit(solution)/shard_map/ppermute | solution.py:538
  135.9 4.4 %collective-permute-done.12 = bf16[2,168,128]{2,1,0:T(8,128)(2,1)S(1)} collective-permute-done((bf16[2,168,128]{2,1,0:T(8,128)(2,1)S(1)}, bf16[2,168,128]{2,1,0:T(8,128)(2,1)S(1)}, u32[]{:S(2)}, u32[]{:S(2)}) %collective-permute-start.12) | collective-permute-done | bytes 86048 | tf_op jit(solution)/shard_map/ppermute | solution.py:538
  140.5 1.0 pad_maximum_fusion
  141.5 3.9 %collective-permute-done.13 = bf16[1,168,128]{2,1,0:T(8,128)(2,1)S(1)} collective-permute-done((bf16[1,168,128]{2,1,0:T(8,128)(2,1)S(1)}, bf16[1,168,128]{2,1,0:T(8,128)(2,1)S(1)}, u32[]{:S(2)}, u32[]{:S(2)}) %collective-permute-start.13) | collective-permute-done | bytes 43040 | tf_op jit(solution)/shard_map/ppermute | solution.py:538
  146.6 0.7 dynamic-slice_bitcast_fusion
  (47 shorter events, 4.6 us)
Async XLA Ops:
  1.7 11.5 %collective-permute-start = (bf16[8,128,128]{2,1,0:T(8,128)(2,1)S(1)}, bf16[8,128,128]{2,1,0:T(8,128)(2,1)S(1)}, u32[]{:S(2)}, u32[]{:S(2)}) collective-permute-start(bf16[8,128,128]{2,1,0:T(8,128)(2,1)S(1)} %get-tuple-element.100), channel_id=1, source_target_pairs={{4,5},{5,6},{6,7},{7,8},{8,9},{9,10},{10,11},{12,13},{13,14},{14,1... | collective-permute-start | bytes 786440 | tf_op jit(solution)/shard_map/ppermute | solution.py:582
  4.1 15.2 %collective-permute-start.1 = (bf16[8,128,128]{2,1,0:T(8,128)(2,1)S(1)}, bf16[8,128,128]{2,1,0:T(8,128)(2,1)S(1)}, u32[]{:S(2)}, u32[]{:S(2)}) collective-permute-start(bf16[8,128,128]{2,1,0:T(8,128)(2,1)S(1)} %get-tuple-element.99), channel_id=1, source_target_pairs={{5,4},{6,5},{7,6},{8,7},{9,8},{10,9},{11,10},{13,12},{14,13},{15,1... | collective-permute-start | bytes 786440 | tf_op jit(solution)/shard_map/ppermute | solution.py:583
  18.2 17.7 %collective-permute-start.3 = (bf16[1024,128]{1,0:T(8,128)(2,1)}, bf16[1024,128]{1,0:T(8,128)(2,1)S(1)}, u32[]{:S(2)}, u32[]{:S(2)}) collective-permute-start(bf16[1024,128]{1,0:T(8,128)(2,1)} %get-tuple-element.52), channel_id=1, source_target_pairs={{0,8},{1,9},{2,10},{3,11},{4,12},{5,13},{6,14},{7,15},{8,0},{9,1},... | collective-permute-start | bytes 786440 | tf_op jit(solution)/shard_map/ppermute | solution.py:589
  24.2 0.8 copy-start
  25.0 0.7 copy-start.2
  25.7 16.9 %collective-permute-start.2 = (bf16[1024,128]{1,0:T(8,128)(2,1)}, bf16[1024,128]{1,0:T(8,128)(2,1)S(1)}, u32[]{:S(2)}, u32[]{:S(2)}) collective-permute-start(bf16[1024,128]{1,0:T(8,128)(2,1)} %get-tuple-element.53), channel_id=1, source_target_pairs={{0,8},{1,9},{2,10},{3,11},{4,12},{5,13},{6,14},{7,15},{8,0},{9,1},... | collective-permute-start | bytes 786440 | tf_op jit(solution)/shard_map/ppermute | solution.py:589
  74.5 11.4 %collective-permute-start.6 = (bf16[512,128]{1,0:T(8,128)(2,1)S(1)}, bf16[512,128]{1,0:T(8,128)(2,1)S(1)}, u32[]{:S(2)}, u32[]{:S(2)}) collective-permute-start(bf16[512,128]{1,0:T(8,128)(2,1)S(1)} %get-tuple-element.79), channel_id=1, source_target_pairs={{0,8},{1,9},{2,10},{3,11},{4,12},{5,13},{6,14},{7,15},{8,0},{9,1},... | collective-permute-start | bytes 393224 | tf_op jit(solution)/shard_map/ppermute | solution.py:610
  79.9 15.4 %copy-start.1 = (bf16[8,128,256]{2,1,0:T(8,128)(2,1)S(1)}, bf16[8,128,256]{2,1,0:T(8,128)(2,1)}, u32[]{:S(2)}) copy-start(bf16[8,128,256]{2,1,0:T(8,128)(2,1)} %copy-done) | copy-start | bytes 1572868
  79.9 15.4 %copy-start.3 = (bf16[1024,128]{1,0:T(8,128)(2,1)S(1)}, bf16[1024,128]{1,0:T(8,128)(2,1)}, u32[]{:S(2)}) copy-start(bf16[1024,128]{1,0:T(8,128)(2,1)} %copy-done.2) | copy-start | bytes 786436
  79.9 15.3 %collective-permute-start.7 = (bf16[512,128]{1,0:T(8,128)(2,1)S(1)}, bf16[512,128]{1,0:T(8,128)(2,1)S(1)}, u32[]{:S(2)}, u32[]{:S(2)}) collective-permute-start(bf16[512,128]{1,0:T(8,128)(2,1)S(1)} %get-tuple-element.80), channel_id=1, source_target_pairs={{0,8},{1,9},{2,10},{3,11},{4,12},{5,13},{6,14},{7,15},{8,0},{9,1},... | collective-permute-start | bytes 393224 | tf_op jit(solution)/shard_map/ppermute | solution.py:610
  82.9 18.9 %collective-permute-start.4 = (bf16[512,128]{1,0:T(8,128)(2,1)S(1)}, bf16[512,128]{1,0:T(8,128)(2,1)S(1)}, u32[]{:S(2)}, u32[]{:S(2)}) collective-permute-start(bf16[512,128]{1,0:T(8,128)(2,1)S(1)} %get-tuple-element.73), channel_id=1, source_target_pairs={{0,8},{1,9},{2,10},{3,11},{4,12},{5,13},{6,14},{7,15},{8,0},{9,1},... | collective-permute-start | bytes 393224 | tf_op jit(solution)/shard_map/ppermute | solution.py:610
  82.9 18.9 %collective-permute-start.5 = (bf16[512,128]{1,0:T(8,128)(2,1)S(1)}, bf16[512,128]{1,0:T(8,128)(2,1)S(1)}, u32[]{:S(2)}, u32[]{:S(2)}) collective-permute-start(bf16[512,128]{1,0:T(8,128)(2,1)S(1)} %get-tuple-element.74), channel_id=1, source_target_pairs={{0,8},{1,9},{2,10},{3,11},{4,12},{5,13},{6,14},{7,15},{8,0},{9,1},... | collective-permute-start | bytes 393224 | tf_op jit(solution)/shard_map/ppermute | solution.py:610
  101.1 0.7 copy-start.4
  112.8 10.2 %copy-start.5 = (bf16[1024,128]{1,0:T(8,128)(2,1)S(1)}, bf16[1024,128]{1,0:T(8,128)(2,1)}, u32[]{:S(2)}) copy-start(bf16[1024,128]{1,0:T(8,128)(2,1)} %copy-done.4) | copy-start | bytes 786436
  118.3 6.7 %collective-permute-start.10 = (bf16[8,168,128]{2,1,0:T(8,128)(2,1)S(1)}, bf16[8,168,128]{2,1,0:T(8,128)(2,1)S(1)}, u32[]{:S(2)}, u32[]{:S(2)}) collective-permute-start(bf16[8,168,128]{2,1,0:T(8,128)(2,1)S(1)} %fusion), channel_id=1, source_target_pairs={{0,1},{1,0},{2,3},{3,2},{4,5},{5,4},{6,7},{7,6},{8,9},{9,8},{10,11... | collective-permute-start | bytes 1032200 | tf_op jit(solution)/shard_map/ppermute | solution.py:538
  118.4 8.6 %collective-permute-start.9 = (bf16[1024,128]{1,0:T(8,128)(2,1)S(1)}, bf16[1024,128]{1,0:T(8,128)(2,1)S(1)}, u32[]{:S(2)}, u32[]{:S(2)}) collective-permute-start(bf16[1024,128]{1,0:T(8,128)(2,1)S(1)} %get-tuple-element.83), channel_id=1, source_target_pairs={{5,4},{6,5},{7,6},{8,7},{9,8},{10,9},{11,10},{13,12},{14,13},{15,1... | collective-permute-start | bytes 786440 | tf_op jit(solution)/shard_map/ppermute | solution.py:622
  123.1 12.8 %collective-permute-start.8 = (bf16[1024,128]{1,0:T(8,128)(2,1)S(1)}, bf16[1024,128]{1,0:T(8,128)(2,1)S(1)}, u32[]{:S(2)}, u32[]{:S(2)}) collective-permute-start(bf16[1024,128]{1,0:T(8,128)(2,1)S(1)} %copy-done.5), channel_id=1, source_target_pairs={{4,5},{5,6},{6,7},{7,8},{8,9},{9,10},{10,11},{12,13},{13,14},{14,1... | collective-permute-start | bytes 786440 | tf_op jit(solution)/shard_map/ppermute | solution.py:622
  126.5 9.2 %collective-permute-start.11 = (bf16[4,168,128]{2,1,0:T(8,128)(2,1)S(1)}, bf16[4,168,128]{2,1,0:T(8,128)(2,1)S(1)}, u32[]{:S(2)}, u32[]{:S(2)}) collective-permute-start(bf16[4,168,128]{2,1,0:T(8,128)(2,1)S(1)} %fusion.3), channel_id=1, source_target_pairs={{0,2},{1,3},{2,0},{3,1},{4,6},{5,7},{6,4},{7,5},{8,10},{9,11},{10,... | collective-permute-start | bytes 516104 | tf_op jit(solution)/shard_map/ppermute | solution.py:538
  135.8 4.6 %collective-permute-start.12 = (bf16[2,168,128]{2,1,0:T(8,128)(2,1)S(1)}, bf16[2,168,128]{2,1,0:T(8,128)(2,1)S(1)}, u32[]{:S(2)}, u32[]{:S(2)}) collective-permute-start(bf16[2,168,128]{2,1,0:T(8,128)(2,1)S(1)} %fusion.7), channel_id=1, source_target_pairs={{0,4},{1,5},{2,6},{3,7},{4,0},{5,1},{6,2},{7,3},{8,12},{9,13},{10,... | collective-permute-start | bytes 258056 | tf_op jit(solution)/shard_map/ppermute | solution.py:538
  140.4 5.0 %collective-permute-start.13 = (bf16[1,168,128]{2,1,0:T(8,128)(2,1)S(1)}, bf16[1,168,128]{2,1,0:T(8,128)(2,1)S(1)}, u32[]{:S(2)}, u32[]{:S(2)}) collective-permute-start(bf16[1,168,128]{2,1,0:T(8,128)(2,1)S(1)} %fusion.9), channel_id=1, source_target_pairs={{0,8},{1,9},{2,10},{3,11},{4,12},{5,13},{6,14},{7,15},{8,0},{9,1},... | collective-permute-start | bytes 129032 | tf_op jit(solution)/shard_map/ppermute | solution.py:538

commit v2 on v1

--- a/solution.py
+++ b/solution.py
@@ -18,9 +18,10 @@
 DENSITY_COEF = 0.3989422804014327
 LOG2_E = 1.4426950408889634
 SCALE = D ** (-0.5)
-
-
-LOCAL_LIMIT = pltpu.CompilerParams(vmem_limit_bytes=20 * 2**20)
+PIECE = 256
+
+
+LOCAL_LIMIT = pltpu.CompilerParams(vmem_limit_bytes=28 * 2**20)
 
 F32 = jnp.float32
 BF16 = jnp.bfloat16
@@ -75,19 +76,26 @@
     return forward, back
 
 
+def whereabouts(offsets_ref, place_ref, count, group):
+    half = count // 2
+    image_place = lax.rem(place_ref[0] + (count - count // 4), count)
+    inside = lax.rem(image_place, half) != (0, half - 1)[group]
+    return offsets_ref[lax.div(image_place, half)], inside
+
+
 def pick(ref, cols, lanes):
     block = ref[:, cols, lanes]
     return block.reshape(block.shape[0] * block.shape[1], block.shape[2])
 
 
 def self_forward_kernel(
-    scal_ref, own_ref, halo_ref, project_ref, merge_ref, gains_ref,
+    offsets_ref, place_ref, own_ref, halo_ref, project_ref, merge_ref, gains_ref,
     middle_ref, mix_ref, qkv_ref, halo_kv_ref, own_rolled, halo_rolled, mix_rolled,
-    *, valid_slot,
+    *, count, group,
 ):
     rows, cols = own_ref.shape[0], own_ref.shape[1]
-    forward, back = roll_matrices(scal_ref[0], cols)
-    valid = scal_ref[valid_slot] > 0
+    offset, valid = whereabouts(offsets_ref, place_ref, count, group)
+    forward, back = roll_matrices(offset, cols)
     for r in range(rows):
         own_rolled[r] = dot_nn(forward, own_ref[r]).astype(BF16)
         halo_rolled[r] = dot_nn(forward, halo_ref[r]).astype(BF16)
@@ -129,13 +137,16 @@
     return pl.BlockSpec(shape, lambda *_: zeros)
 
 
-def self_forward(group, scal, features, halo, self_project, self_merge, norm_gains):
+def self_forward(group, offsets, place, features, halo, self_project, self_merge, norm_gains):
     rows, cols, _ = halo.shape
     tokens = rows * cols
     return pl.pallas_call(
-        functools.partial(self_forward_kernel, valid_slot=1 + group),
+        functools.partial(
+            self_forward_kernel, count=lax.axis_size("tiles"), group=group
+        ),
         grid=(1,),
         in_specs=[
+            pl.BlockSpec(memory_space=pltpu.SMEM),
             pl.BlockSpec(memory_space=pltpu.SMEM),
             pl.BlockSpec((rows, cols, D), lambda i: (group, 0, 0)),
             full_spec(halo.shape),
@@ -158,79 +169,128 @@
         scratch_shapes=[pltpu.VMEM((rows, cols, D), BF16)] * 3,
         compiler_params=LOCAL_LIMIT,
         name="self_forward",
-    )(scal, features, halo, self_project, self_merge, norm_gains)
-
-
-def cross_open_kernel(middle_ref, partner_ref, project_ref, q_ref, kv_ref, mix_ref, stat_ref):
-    @pl.when(pl.program_id(0) == 0)
+    )(offsets, place, features, halo, self_project, self_merge, norm_gains)
+
+
+def key_scores(kv_ref, q):
+    return dot_nt(kv_ref[:, :D], q) * (SCALE * LOG2_E)
+
+
+def cross_open_kernel(
+    low_ref, high_ref, partner_ref, project_ref,
+    middle_ref, q_ref, kv_ref, mix_ref, stat_ref, raised_ref, values_t,
+):
+    step = pl.program_id(0)
+    block = low_ref.shape[0]
+
+    @pl.when(step == 0)
     def _():
         kv_ref[...] = dot_nn(partner_ref[...], project_ref[:, D:]).astype(BF16)
-
-    q = dot_nn(middle_ref[...], project_ref[:, :D]).astype(BF16)
+        values_t[...] = kv_ref[:, D:].T
+
+    middle = jnp.where(step < pl.num_programs(0) // 2, low_ref[...], high_ref[...])
+    middle_ref[...] = middle
+    q = dot_nn(middle, project_ref[:, :D]).astype(BF16)
     q_ref[...] = q
-    logits = dot_nt(q, kv_ref[:, :D]) * (SCALE * LOG2_E)
-    top = jnp.max(logits, axis=-1, keepdims=True)
-    raised = jnp.exp2(logits - top)
-    total = jnp.sum(raised, axis=-1, keepdims=True)
-    mix_ref[...] = dot_nn(raised.astype(BF16), kv_ref[:, D:])
-    lane = lax.broadcasted_iota(jnp.int32, stat_ref.shape, 1)
-    stat_ref[...] = jnp.where(lane == 0, top, total)
-
-
-def cross_open(block, middles, partner, cross_project):
+    base = pl.multiple_of(step * block, block)
+    row = lax.broadcasted_iota(jnp.int32, (stat_ref.shape[0], PIECE), 0)
+    logits = key_scores(kv_ref, q[:PIECE])
+    for start in range(0, block, PIECE):
+        span = slice(start, start + PIECE)
+        current = logits
+        if start + PIECE < block:
+            logits = key_scores(kv_ref, q[start + PIECE : start + 2 * PIECE])
+        top = jnp.max(current, axis=0, keepdims=True)
+        raised = jnp.exp2(current - top)
+        total = jnp.sum(raised, axis=0, keepdims=True)
+        packed = raised.astype(BF16)
+        raised_ref[:, pl.ds(base + start, PIECE)] = packed
+        mix_ref[:, span] = dot_nn(values_t[...], packed)
+        stat_ref[:, span] = jnp.where(row == 0, top, total)
+
+
+def cross_open(block, low, high, partner, cross_project):
     chunk = partner.shape[0]
-    tokens = middles.shape[0]
+    half = low.shape[0]
+    tokens = 2 * half
+    steps = tokens // block
     row = lambda i: (i, 0)
+    column = lambda i: (0, i)
     return pl.pallas_call(
         cross_open_kernel,
-        grid=(tokens // block,),
+        grid=(steps,),
         in_specs=[
-            pl.BlockSpec((block, D), row),
+            pl.BlockSpec((block, D), lambda i: (jnp.minimum(i, steps // 2 - 1), 0)),
+            pl.BlockSpec((block, D), lambda i: (jnp.maximum(i - steps // 2, 0), 0)),
             full_spec(partner.shape),
             full_spec(cross_project.shape),
         ],
         out_specs=[
             pl.BlockSpec((block, D), row),
+            pl.BlockSpec((block, D), row),
             full_spec((chunk, 2 * D)),
-            pl.BlockSpec((block, D), row),
-            pl.BlockSpec((block, D), row),
+            pl.BlockSpec((D, block), column),
+            pl.BlockSpec((8, block), column),
+            pl.BlockSpec(memory_space=pltpu.VMEM),
         ],
         out_shape=[
             jax.ShapeDtypeStruct((tokens, D), BF16),
+            jax.ShapeDtypeStruct((tokens, D), BF16),
             jax.ShapeDtypeStruct((chunk, 2 * D), BF16),
-            jax.ShapeDtypeStruct((tokens, D), F32),
-            jax.ShapeDtypeStruct((tokens, D), F32),
-        ],
+            jax.ShapeDtypeStruct((D, tokens), F32),
+            jax.ShapeDtypeStruct((8, tokens), F32),
+            pltpu.VMEM((chunk, tokens), BF16),
+        ],
+        scratch_shapes=[pltpu.VMEM((D, chunk), BF16)],
         compiler_params=LOCAL_LIMIT,
         name="cross_open",
-    )(middles, partner, cross_project)
+    )(low, high, partner, cross_project)
 
 
 def cross_close_kernel(
     middle_ref, partner_ref, project_ref, q_ref, open_mix_ref, open_stat_ref,
     merge_ref, feed_in_ref, feed_out_ref, gains_ref, upstream_ref,
     kv_ref, result_ref, mid_grad_ref, mix_grad_ref, stat_ref,
-    grad_in_ref, grad_out_ref, grad_merge_ref, grad_gain_ref,
+    grad_in_ref, grad_out_ref, grad_merge_ref, grad_gain_ref, raised_ref,
+    values_t, grad_out_t,
 ):
-    @pl.when(pl.program_id(0) == 0)
+    step = pl.program_id(0)
+    block = middle_ref.shape[0]
+
+    @pl.when(step == 0)
     def _():
         kv_ref[...] = dot_nn(partner_ref[...], project_ref[:, D:]).astype(BF16)
+        values_t[...] = kv_ref[:, D:].T
         grad_in_ref[...] = jnp.zeros_like(grad_in_ref)
-        grad_out_ref[...] = jnp.zeros_like(grad_out_ref)
+        grad_out_t[...] = jnp.zeros_like(grad_out_t)
         grad_merge_ref[...] = jnp.zeros_like(grad_merge_ref)
         grad_gain_ref[...] = jnp.zeros_like(grad_gain_ref)
 
-    block = middle_ref.shape[0]
-    logits = dot_nt(q_ref[...], kv_ref[:, :D]) * (SCALE * LOG2_E)
-    open_top = open_stat_ref[:, 0:1]
-    open_total = open_stat_ref[:, 1:2]
-    top = jnp.maximum(jnp.max(logits, axis=-1, keepdims=True), open_top)
-    raised = jnp.exp2(logits - top)
-    carry = jnp.exp2(open_top - top)
-    total = jnp.sum(raised, axis=-1, keepdims=True) + open_total * carry
-    mixed = dot_nn(raised.astype(BF16), kv_ref[:, D:]) + open_mix_ref[...] * carry
-    mixed = mixed * (1.0 / total)
-    log_total = top + jnp.log2(total)
+    base = pl.multiple_of(step * block, block)
+    pieces, first_factors, second_factors = [], [], []
+    logits = key_scores(kv_ref, q_ref[:PIECE, :])
+    for start in range(0, block, PIECE):
+        span = slice(start, start + PIECE)
+        current = logits
+        if start + PIECE < block:
+            logits = key_scores(kv_ref, q_ref[start + PIECE : start + 2 * PIECE, :])
+        open_top = open_stat_ref[0:1, span]
+        top = jnp.maximum(jnp.max(current, axis=0, keepdims=True), open_top)
+        raised = jnp.exp2(current - top)
+        carry = jnp.exp2(open_top - top)
+        total = jnp.sum(raised, axis=0, keepdims=True) + open_stat_ref[1:2, span] * carry
+        packed = raised.astype(BF16)
+        raised_ref[:, pl.ds(base + start, PIECE)] = packed
+        inverse_total = 1.0 / total
+        pieces.append(
+            (dot_nn(values_t[...], packed) + open_mix_ref[:, span] * carry) * inverse_total
+        )
+        first_factors.append(carry * inverse_total)
+        second_factors.append(inverse_total)
+    mixed = jnp.concatenate(pieces, axis=1)
+    first_factor = jnp.concatenate(first_factors, axis=1)
+    second_factor = jnp.concatenate(second_factors, axis=1)
+    mixed = mixed.T
     cross_mix = mixed.astype(BF16)
 
     middle = middle_ref[...]
@@ -260,7 +320,7 @@
     for b in range(lanes):
         grad_in_ref[b, :D, :] += grad_low[:, b * D : (b + 1) * D]
         grad_in_ref[b, D:, :] += grad_high[:, b * D : (b + 1) * D]
-    grad_out_ref[...] += dot_tn(hidden, grad_post)
+    grad_out_t[...] += dot_tn(grad_post, hidden)
     merged_full, gain_grad_cross = norm_backward(
         grad_joined[:, D:], gain_cross, cross_unit, cross_inverse
     )
@@ -269,11 +329,17 @@
     mix_grad = dot_nt(grad_merged, merge_ref[...]).astype(BF16)
     mix_grad_ref[...] = mix_grad
     inner = jnp.sum(mix_grad.astype(F32) * mixed, axis=-1, keepdims=True)
-    lane = lax.broadcasted_iota(jnp.int32, (block, D), 1)
-    stats = jnp.where(lane == 0, log_total, inner)
-    stat_ref[...] = stats.T[: stat_ref.shape[0], :]
+    inner_row = jnp.broadcast_to(inner, (block, D)).T[: stat_ref.shape[0], :]
+    row = lax.broadcasted_iota(jnp.int32, stat_ref.shape, 0)
+    stat_ref[...] = jnp.where(
+        row == 0, inner_row, jnp.where(row == 1, first_factor, second_factor)
+    )
     grad_gain_ref[1:2, :] += gain_grad_cross
     grad_gain_ref[2:3, :] += gain_grad_feed
+
+    @pl.when(step == pl.num_programs(0) - 1)
+    def _():
+        grad_out_ref[...] = grad_out_t[...].T
 
 
 def cross_close(
@@ -283,21 +349,23 @@
     tokens = middles.shape[0]
     chunk = partner.shape[0]
     hidden = feed_in.shape[1]
-    row = lambda i: (i, 0)
-    tile = pl.BlockSpec((block, D), row)
+    tile = pl.BlockSpec((block, D), lambda i: (i, 0))
+    column = lambda i: (0, i)
     return pl.pallas_call(
         cross_close_kernel,
         grid=(tokens // block,),
         in_specs=[
-            tile, full_spec(partner.shape), full_spec(cross_project.shape), tile, tile, tile,
+            tile, full_spec(partner.shape), full_spec(cross_project.shape), tile,
+            pl.BlockSpec((D, block), column), pl.BlockSpec((8, block), column),
             full_spec(cross_merge.shape), full_spec(feed_in.shape), full_spec(feed_out.shape),
             full_spec(norm_gains.shape), tile,
         ],
         out_specs=[
             full_spec((chunk, 2 * D)), tile, tile, tile,
-            pl.BlockSpec((8, block), lambda i: (0, i)),
+            pl.BlockSpec((8, block), column),
             full_spec((hidden // D, 2 * D, D)), full_spec((hidden, D)), full_spec((D, D)),
             full_spec((8, D)),
+            pl.BlockSpec(memory_space=pltpu.VMEM),
         ],
         out_shape=[
             jax.ShapeDtypeStruct((chunk, 2 * D), BF16),
@@ -309,17 +377,19 @@
             jax.ShapeDtypeStruct((hidden, D), F32),
             jax.ShapeDtypeStruct((D, D), F32),
             jax.ShapeDtypeStruct((8, D), F32),
-        ],
+            pltpu.VMEM((chunk, tokens), BF16),
+        ],
+        scratch_shapes=[pltpu.VMEM((D, chunk), BF16), pltpu.VMEM((D, hidden), F32)],
         compiler_params=LOCAL_LIMIT,
         name="cross_close",
     )(middles, partner, cross_project, q, open_mix, open_stat,
       cross_merge, feed_in, feed_out, norm_gains, upstream)
 
 
-def cross_back_kernel(*refs, first, last, q_block):
+def cross_back_kernel(*refs, first, last, q_block, index, factor_row):
     refs = list(refs)
-    q_ref, grad_ref, stat_ref, kv_ref, partner_ref, project_ref = refs[:6]
-    refs = refs[6:]
+    q_ref, grad_ref, stat_ref, raised_ref, kv_ref, partner_ref, project_ref = refs[:7]
+    refs = refs[7:]
     if not first:
         q_in_ref, weight_in_ref = refs[:2]
         refs = refs[2:]
@@ -343,15 +413,16 @@
     keys = kv_ref[:, :D]
     values = kv_ref[:, D:]
     tokens = q_ref.shape[0]
+    block = kv_ref.shape[0]
 
     @pl.loop(0, tokens // q_block)
     def _(j):
         span = pl.ds(pl.multiple_of(j * q_block, q_block), q_block)
         q = q_ref[span, :]
         grad = grad_ref[span, :]
-        log_total = stat_ref[0:1, span]
-        inner = stat_ref[1:2, span]
-        shares = jnp.exp2(dot_nt(keys, q) * (SCALE * LOG2_E) - log_total)
+        inner = stat_ref[0:1, span]
+        factor = stat_ref[factor_row : factor_row + 1, span]
+        shares = raised_ref[index * block : (index + 1) * block, span].astype(F32) * factor
         slopes = dot_nt(values, grad) - inner
         v_acc[...] += dot_nn(shares.astype(BF16), grad)
         logit_grad = (shares * slopes).astype(BF16)
@@ -377,14 +448,15 @@
 
 
 def cross_back(
-    block, index, q_block, q, mix_grad, stats, kv, partner, cross_project,
+    block, index, factor_row, q_block, q, mix_grad, stats, raised, kv, partner, cross_project,
     carried=None, finish=None,
 ):
     tokens = q.shape[0]
     first, last = carried is None, finish is not None
-    args = [q, mix_grad, stats, kv, partner, cross_project]
+    args = [q, mix_grad, stats, on_chip(raised), kv, partner, cross_project]
     specs = [
         full_spec(q.shape), full_spec(mix_grad.shape), full_spec(stats.shape),
+        pl.BlockSpec(memory_space=pltpu.VMEM),
         pl.BlockSpec((block, 2 * D), lambda i: (index, 0)),
         pl.BlockSpec((block, D), lambda i: (index, 0)),
         full_spec(cross_project.shape),
@@ -393,7 +465,10 @@
         args.append(extra)
         specs.append(full_spec(extra.shape))
     return pl.pallas_call(
-        functools.partial(cross_back_kernel, first=first, last=last, q_block=q_block),
+        functools.partial(
+            cross_back_kernel, first=first, last=last, q_block=q_block, index=index,
+            factor_row=factor_row,
+        ),
         grid=(1,),
         in_specs=specs,
         out_specs=[
@@ -413,23 +488,24 @@
 
 
 def self_back_kernel(
-    scal_ref, own_ref, halo_ref, qkv_ref, halo_kv_ref, mix_ref, mid_grad_ref,
+    offsets_ref, place_ref, own_ref, halo_ref, qkv_ref, halo_kv_ref, mix_ref, mid_grad_ref,
     term_low_ref, term_high_ref, project_ref, merge_ref, gains_ref,
     feature_grad_ref, halo_term_ref, weight_ref, merge_grad_ref, gain_ref,
     mix_grad, own_grad, halo_grad, own_back, halo_back,
-    *, valid_slot,
+    *, count, group,
 ):
     rows, cols = own_ref.shape[0], own_ref.shape[1]
     tokens = rows * cols
-    forward, back = roll_matrices(scal_ref[0], cols)
-    valid = scal_ref[valid_slot] > 0
+    offset, valid = whereabouts(offsets_ref, place_ref, count, group)
+    forward, back = roll_matrices(offset, cols)
     upstream = mid_grad_ref[...] + jnp.concatenate(
         [term_low_ref[...].astype(F32), term_high_ref[...].astype(F32)], axis=0
     )
     gain = gains_ref[0:1, :]
     _, unit, inverse = layer_norm(dot_nn(mix_ref[...], merge_ref[...]), gain)
     merged_full, gain_grad = norm_backward(upstream, gain, unit, inverse)
-    gain_ref[...] = jnp.broadcast_to(gain_grad, gain_ref.shape)
+    gain_row = lax.broadcasted_iota(jnp.int32, gain_ref.shape, 0)
+    gain_ref[...] = jnp.where(gain_row == 0, gain_grad, 0.0)
     grad_merged = merged_full.astype(BF16)
     merge_grad_ref[...] = dot_tn(mix_ref[...], grad_merged)
     plain_grad = dot_nt(grad_merged, merge_ref[...]).astype(BF16)
@@ -483,15 +559,18 @@
 
 
 def self_back(
-    group, scal, features, halo, qkv, halo_kv, mix, mid_grad, term_low, term_high,
+    group, offsets, place, features, halo, qkv, halo_kv, mix, mid_grad, term_low, term_high,
     self_project, self_merge, norm_gains,
 ):
     rows, cols, _ = halo.shape
     tokens = rows * cols
     return pl.pallas_call(
-        functools.partial(self_back_kernel, valid_slot=1 + group),
+        functools.partial(
+            self_back_kernel, count=lax.axis_size("tiles"), group=group
+        ),
         grid=(1,),
         in_specs=[
+            pl.BlockSpec(memory_space=pltpu.SMEM),
             pl.BlockSpec(memory_space=pltpu.SMEM),
             pl.BlockSpec((rows, cols, D), lambda i: (group, 0, 0)),
             full_spec(halo.shape), full_spec(qkv.shape), full_spec(halo_kv.shape),
@@ -521,24 +600,101 @@
         ],
         compiler_params=LOCAL_LIMIT,
         name="self_back",
-    )(scal, features, halo, qkv, halo_kv, mix, mid_grad, term_low, term_high,
+    )(offsets, place, features, halo, qkv, halo_kv, mix, mid_grad, term_low, term_high,
       self_project, self_merge, norm_gains)
 
 
-def scattered_sum(pieces, axis):
+def pack_kernel(
+    place_ref, self_a, self_b, merge_a, merge_b, cross_ref, cross_merge_ref, in_ref, out_ref,
+    gain_a, gain_b, gain_c, kept_ref, sent_ref,
+):
+    pairs = kept_ref.shape[0]
+    odd = lax.rem(place_ref[0], 2)
+    sources = [[self_a.at[b], self_b.at[b]] for b in range(self_a.shape[0])]
+    sources += [[merge_a, merge_b]]
+    sources += [[cross_ref.at[b]] for b in range(cross_ref.shape[0])]
+    sources += [[cross_merge_ref]]
+    sources += [[in_ref.at[b]] for b in range(in_ref.shape[0])]
+    sources += [[out_ref]]
+    gains = gain_a[...] + gain_b[...] + gain_c[...]
+    for p in range(pairs):
+        start = 0
+        for refs in sources:
+            size = refs[0].shape[0] // (2 * pairs)
+            kept_rows = pl.ds(pl.multiple_of((2 * p + odd) * size, size), size)
+            sent_rows = pl.ds(pl.multiple_of((2 * p + 1 - odd) * size, size), size)
+            kept = refs[0][kept_rows, :]
+            sent = refs[0][sent_rows, :]
+            for ref in refs[1:]:
+                kept = kept + ref[kept_rows, :]
+                sent = sent + ref[sent_rows, :]
+            kept_ref[p, start : start + size, :] = kept
+            sent_ref[p, start : start + size, :] = sent.astype(BF16)
+            start += size
+        kept_ref[p, start : start + gains.shape[0], :] = gains
+        sent_ref[p, start : start + gains.shape[0], :] = gains.astype(BF16)
+
+
+def pack(count, place, *arrays):
+    rows = sum(math.prod(a.shape[:-1]) for a in arrays) // count
+    rows -= sum(math.prod(arrays[i].shape[:-1]) for i in (1, 3)) // count
+    rows -= sum(math.prod(a.shape[:-1]) for a in arrays[-3:]) // count
+    rows += arrays[-1].shape[0]
+    shape = (count // 2, rows, D)
+    whole = pl.BlockSpec(memory_space=pltpu.VMEM)
+    return pl.pallas_call(
+        pack_kernel,
+        in_specs=[pl.BlockSpec(memory_space=pltpu.SMEM)] + [whole] * len(arrays),
+        out_specs=[whole, whole],
+        out_shape=[jax.ShapeDtypeStruct(shape, F32), jax.ShapeDtypeStruct(shape, BF16)],
+        compiler_params=LOCAL_LIMIT,
+        name="pack",
+    )(place, *arrays)
+
+
+def unpack_kernel(place_ref, kept_ref, got_ref, *outs, scale):
+    start = 0
+    for out in outs[:-1]:
+        size = out.shape[0]
+        for b in range(out.shape[1] // D):
+            rows = slice(start, start + size)
+            out[:, b * D : (b + 1) * D] = (
+                kept_ref[0, rows, :] + got_ref[0, rows, :].astype(F32)
+            ) * scale
+            start += size
+    gains_out = outs[-1]
+    lanes = gains_out.shape[1]
+    rows = slice(start, start + 8)
+    gains = (kept_ref[0, rows, :] + got_ref[0, rows, :].astype(F32)) * scale
+    shift = lax.rem(D - place_ref[0] * lanes, D)
+    gains_out[...] = pltpu.roll(gains, shift, 1)[: gains_out.shape[0], :lanes]
+
+
+def unpack(place, kept, got, shapes, scale):
+    whole = pl.BlockSpec(memory_space=pltpu.VMEM)
+    return pl.pallas_call(
+        functools.partial(unpack_kernel, scale=scale),
+        in_specs=[pl.BlockSpec(memory_space=pltpu.SMEM), whole, whole],
+        out_specs=[whole] * len(shapes),
+        out_shape=[jax.ShapeDtypeStruct(shape, F32) for shape in shapes],
+        compiler_params=LOCAL_LIMIT,
+        name="unpack",
+    )(place, kept, got)
+
+
+def scattered_halves(kept, sent, axis):
     count = lax.axis_size(axis)
-    place = lax.axis_index(axis)
-    current = pieces
+    index = lax.axis_index(axis)
     bit = 1
-    while bit < count:
-        pairs = current.reshape((current.shape[0] // 2, 2) + current.shape[1:])
-        odd = (place & bit) != 0
+    while True:
+        got = lax.ppermute(sent, axis, [(i, i ^ bit) for i in range(count)])
+        if kept.shape[0] == 1:
+            return kept, got
+        bit *= 2
+        pairs = (kept + got.astype(F32)).reshape((kept.shape[0] // 2, 2) + kept.shape[1:])
+        odd = (index & bit) != 0
         kept = jnp.where(odd, pairs[:, 1], pairs[:, 0])
         sent = jnp.where(odd, pairs[:, 0], pairs[:, 1]).astype(BF16)
-        got = lax.ppermute(sent, axis, [(i, i ^ bit) for i in range(count)])
-        current = kept + got.astype(F32)
-        bit *= 2
-    return current[0]
 
 
 def body(
@@ -552,15 +708,8 @@
     count = lax.axis_size("tiles")
     half_tiles = count // 2
     shift = count // 4
-    position = lax.axis_index("tiles")
-    image_place = (position + count - shift) % count
-    offset = window_offsets[image_place // half_tiles]
+    place = lax.axis_index("tiles").astype(jnp.int32).reshape(1)
     grad_scale = 1.0 / math.sqrt(count * tile_tokens)
-    upper_valid = image_place % half_tiles != 0
-    lower_valid = image_place % half_tiles != half_tiles - 1
-    scal = jnp.stack(
-        [offset, upper_valid.astype(jnp.int32), lower_valid.astype(jnp.int32)]
-    )
     inner = [
         ((i + shift) % count, (i + 1 + shift) % count)
         for i in range(count)
@@ -583,16 +732,18 @@
         lax.ppermute(raw_features[:half_rows], "tiles", to_previous),
     )
     parts = [
-        self_forward(g, scal, features, halos[g], self_project, self_merge, norm_gains)
+        self_forward(g, window_offsets, place, features, halos[g], self_project, self_merge, norm_gains)
         for g in range(2)
     ]
     partners = [lax.ppermute(parts[g][0], "tiles", to_partner) for g in range(2)]
-    middles = jnp.concatenate([parts[0][0], parts[1][0]], axis=0)
-
-    block = min(512, half_tokens)
+
+    block = min(1024, half_tokens)
     upstream = off_chip(result_grad.reshape(tile_tokens, D))
-    q, kv_a, open_mix, open_stat = cross_open(block, middles, partners[0], cross_project)
-    (kv_b, result, mid_grad, mix_grad, stats, grad_in, grad_out, grad_merge, gain_grad) = (
+    middles, q, kv_a, open_mix, open_stat, raised_a = cross_open(
+        block, parts[0][0], parts[1][0], partners[0], cross_project
+    )
+    (kv_b, result, mid_grad, mix_grad, stats, grad_in, grad_out, grad_merge, gain_grad,
+     raised_b) = (
         cross_close(
             block, middles, partners[1], cross_project, q, open_mix, open_stat,
             cross_merge, feed_in, feed_out, norm_gains, upstream,
@@ -602,7 +753,8 @@
     carried, got = None, []
     for c in range(4):
         term, q_grad, cross_weight = cross_back(
-            half, c % 2, block, q, mix_grad, stats, (kv_a, kv_b)[c // 2],
+            half, c % 2, 1 + c // 2, half, q, mix_grad, stats,
+            (raised_a, raised_b)[c // 2], (kv_a, kv_b)[c // 2],
             partners[c // 2], cross_project,
             carried=carried, finish=(mid_grad, middles) if c == 3 else None,
         )
@@ -613,7 +765,7 @@
     for g in range(2):
         backs.append(
             self_back(
-                g, scal, features, halos[g],
+                g, window_offsets, place, features, halos[g],
                 on_chip(parts[g][2]), on_chip(parts[g][3]), on_chip(parts[g][1]),
                 mid_grad, got[2 * g], got[2 * g + 1], self_project, self_merge, norm_gains,
             )
@@ -630,54 +782,26 @@
         axis=0,
     ).reshape(tile_rows, tile_cols, D)
 
-    self_weight = backs[0][2] + backs[1][2]
-    merge_weight = backs[0][3] + backs[1][3]
-    gains = jnp.concatenate(
-        [backs[0][4][0:1] + backs[1][4][0:1], gain_grad[1:8]], axis=0
-    )
-
-    def cut(array):
-        return array.reshape(count, array.shape[0] // count, D)
-
-    summed = scattered_sum(
-        jnp.concatenate(
-            [cut(self_weight[b]) for b in range(3)]
-            + [cut(merge_weight)]
-            + [cut(cross_weight[b]) for b in range(3)]
-            + [cut(grad_merge)]
-            + [cut(grad_in[b]) for b in range(grad_in.shape[0])]
-            + [cut(grad_out)]
-            + [jnp.broadcast_to(gains[None], (count,) + gains.shape)],
-            axis=1,
+    kept, got_last = scattered_halves(
+        *pack(
+            count, place, backs[0][2], backs[1][2], backs[0][3], backs[1][3], cross_weight,
+            grad_merge, grad_in, grad_out, backs[0][4], backs[1][4], gain_grad,
         ),
         "tiles",
-    ) * grad_scale
-    place = 0
-
-    def take(rows, blocks):
-        nonlocal place
-        found = [summed[place + b * rows : place + (b + 1) * rows] for b in range(blocks)]
-        place += rows * blocks
-        return jnp.concatenate(found, axis=1)
-
-    out_self = take(D // count, 3)
-    out_self_merge = take(D // count, 1)
-    out_cross = take(D // count, 3)
-    out_cross_merge = take(D // count, 1)
-    out_in = take(2 * D // count, feed_in.shape[1] // D)
-    out_out = take(feed_out.shape[0] // count, 1)
-    lanes = D // count
-    out_gains = lax.dynamic_slice(summed[place : place + 3], (0, position * lanes), (3, lanes))
+    )
+    grads = unpack(
+        place, kept, got_last,
+        [
+            (D // count, 3 * D), (D // count, D), (D // count, 3 * D), (D // count, D),
+            (2 * D // count, feed_in.shape[1]), (feed_out.shape[0] // count, D),
+            (norm_gains.shape[0], D // count),
+        ],
+        grad_scale,
+    )
     return (
         result.reshape(tile_rows, tile_cols, D),
         features_grad,
-        out_self,
-        out_self_merge,
-        out_cross,
-        out_cross_merge,
-        out_in,
-        out_out,
-        out_gains,
+        *grads,
     )
 
 

time: 149 us -> 128 us (0.86)
  local copies, waits for them, and re-layouts: 17.6 us -> 1.72 us
  Pallas kernels: 65.5 us -> 58.4 us
  waiting for transfers between devices: 32.8 us -> 37.5 us
  other arithmetic: 6.05 us -> 1.36 us
  starting transfers between devices: 25.5 us -> 27.6 us
    unnamed x26 -> x2, local copies, waits for them, and re-layouts: 11.8 us -> 0.66 us
    ppermute x4, waiting for transfers between devices: 16.9 us -> 11.2 us  [scattered_halves(): got = lax.ppermute(sent, axis, [(i, i ^ bit) for i in range(count)])]
    ppermute x2, waiting for transfers between devices: 0.01 us -> 5.11 us  [body(): terms.append(lax.ppermute(backs[g][1], 'tiles', (to_previous, to_next)[g]))]
    pallas_call x1, Pallas kernels: 17.5 us -> 13.4 us  [cross_close(): pl.pallas_call(cross_close_kernel, grid=(tokens // block,), in_specs=[til...]
    ppermute x4, starting transfers between devices: 0.76 us -> 3.92 us  [scattered_halves(): got = lax.ppermute(sent, axis, [(i, i ^ bit) for i in range(count)])]
    ppermute x2, waiting for transfers between devices: 6.33 us -> 8.49 us  [body(): lax.ppermute(parts[g][0], 'tiles', to_partner)]
    ppermute x1, waiting for transfers between devices: 0.2 us -> 2.21 us  [body(): lax.ppermute(raw_features[half_rows:], 'tiles', to_next)]
    dynamic_slice x2 -> x0, local copies, waits for them, and re-layouts: 1.89 us -> none  [the longest x1 1.24 us: body(): offset = window_offsets[image_place // half_tiles]]
  transfers between devices with their start and end apart: 14 -> 14, of which waited for: 6 -> 8; matrix products, arithmetic and copies ran while one was open for 4% -> 1% of each run, Pallas kernels for 19% -> 27%
where the time goes in v2:
time: 128 us; the launch traced here: 127 us
  Pallas kernels  58.4 us (46%)
  waiting for transfers between devices  37.5 us (29%)
  starting transfers between devices  27.6 us (22%)
  local copies, waits for them, and re-layouts  1.72 us (1%)
  other arithmetic  1.36 us (1%)
    pallas_call x4, Pallas kernels, cross_back(): pl.pallas_call(functools.partial(cross_back_kernel, first=first, last=las...  17.9 us
    pallas_call x1, Pallas kernels, cross_close(): pl.pallas_call(cross_close_kernel, grid=(tokens // block,), in_specs=[til...  13.4 us
    pallas_call x2, Pallas kernels, self_back(): pl.pallas_call(functools.partial(self_back_kernel, count=lax.axis_size('t...  11.7 us
    ppermute x4, waiting for transfers between devices, scattered_halves(): got = lax.ppermute(sent, axis, [(i, i ^ bit) for i in range(count)])  11.2 us
    ppermute x4, waiting for transfers between devices, body(): got.append(lax.ppermute(term, 'tiles', to_partner))  10.6 us
    ppermute x2, waiting for transfers between devices, body(): lax.ppermute(parts[g][0], 'tiles', to_partner)  8.49 us
    pallas_call x2, Pallas kernels, self_forward(): pl.pallas_call(functools.partial(self_forward_kernel, count=lax.axis_size...  8.42 us
    ppermute x1, starting transfers between devices, body(): lax.ppermute(raw_features[:half_rows], 'tiles', to_previous)  6.9 us
  transfers between devices with their start and end apart: 14, of which 8 were waited for; matrix products, arithmetic and copies ran while one was open for 1% of the time, Pallas kernels for 27%

profile of v2, /device:TPU:0, one launch (start us, length us, event | category | flops | bytes accessed | tf_op | source)
XLA Modules:
  0.0 127.5 jit_solution(13191640085338118232)
XLA Ops:
  0.6 1.1 fusion.4
  1.7 2.4 %collective-permute-start = (bf16[8,128,128]{2,1,0:T(8,128)(2,1)S(1)}, bf16[8,128,128]{2,1,0:T(8,128)(2,1)S(1)}, u32[]{:S(2)}, u32[]{:S(2)}) collective-permute-start(bf16[8,128,128]{2,1,0:T(8,128)(2,1)S(1)} %get-tuple-element.120), channel_id=1, source_target_pairs={{4,5},{5,6},{6,7},{7,8},{8,9},{9,10},{10,11},{12,13},{13,14},{14,1... | collective-permute-start | bytes 786440 | tf_op jit(solution)/shard_map/ppermute | solution.py:731
  4.1 6.9 %collective-permute-start.1 = (bf16[8,128,128]{2,1,0:T(8,128)(2,1)S(1)}, bf16[8,128,128]{2,1,0:T(8,128)(2,1)S(1)}, u32[]{:S(2)}, u32[]{:S(2)}) collective-permute-start(bf16[8,128,128]{2,1,0:T(8,128)(2,1)S(1)} %get-tuple-element.119), channel_id=1, source_target_pairs={{5,4},{6,5},{7,6},{8,7},{9,8},{10,9},{11,10},{13,12},{14,13},{15,1... | collective-permute-start | bytes 786440 | tf_op jit(solution)/shard_map/ppermute | solution.py:732
  11.0 2.2 %collective-permute-done.halo_ref = bf16[8,128,128]{2,1,0:T(8,128)(2,1)S(1)} collective-permute-done((bf16[8,128,128]{2,1,0:T(8,128)(2,1)S(1)}, bf16[8,128,128]{2,1,0:T(8,128)(2,1)S(1)}, u32[]{:S(2)}, u32[]{:S(2)}) %collective-permute-start) | collective-permute-done | bytes 262176 | tf_op jit(solution)/shard_map/ppermute | solution.py:731
  13.2 0.0 copy-start
  13.2 0.7 copy-done
  13.9 4.2 %self_forward.2 = (bf16[1024,128]{1,0:T(8,128)(2,1)S(1)}, bf16[1024,128]{1,0:T(8,128)(2,1)S(1)}, bf16[8,128,384]{2,1,0:T(8,128)(2,1)S(1)}, bf16[8,128,256]{2,1,0:T(8,128)(2,1)S(1)}) custom-call(s32[2]{0:T(128)S(1)} %copy-done, s32[1]{0:T(128)} %bitcast.place_ref, bf16[16,128,128]{2,1,0:T(8,128)(2,1)} %own_ref.7, ...), custom_call_target="tpu_custom_call" | custom-call | tf_op jit(solution)/shard_map/self_forward/pallas_call | solution.py:143
  18.1 1.2 collective-permute-start.2
  19.3 0.0 collective-permute-done.1.halo_ref
  19.3 4.2 %self_forward.3 = (bf16[1024,128]{1,0:T(8,128)(2,1)S(1)}, bf16[1024,128]{1,0:T(8,128)(2,1)S(1)}, bf16[8,128,384]{2,1,0:T(8,128)(2,1)S(1)}, bf16[8,128,256]{2,1,0:T(8,128)(2,1)S(1)}) custom-call(s32[2]{0:T(128)S(1)} %copy-done, s32[1]{0:T(128)} %bitcast.place_ref, bf16[16,128,128]{2,1,0:T(8,128)(2,1)} %own_ref.7, ...), custom_call_target="tpu_custom_call" | custom-call | tf_op jit(solution)/shard_map/self_forward/pallas_call | solution.py:143
  23.5 1.9 %collective-permute-start.3 = (bf16[1024,128]{1,0:T(8,128)(2,1)S(1)}, bf16[1024,128]{1,0:T(8,128)(2,1)S(1)}, u32[]{:S(2)}, u32[]{:S(2)}) collective-permute-start(bf16[1024,128]{1,0:T(8,128)(2,1)S(1)} %get-tuple-element.65.high_ref), channel_id=1, source_target_pairs={{0,8},{1,9},{2,10},{3,11},{4,12},{5,13},{6,14},{7,15},{8,0},{9,1},... | collective-permute-start | bytes 786440 | tf_op jit(solution)/shard_map/ppermute | solution.py:738
  25.4 8.5 %collective-permute-done.2.partner_ref.refs_5_ = bf16[1024,128]{1,0:T(8,128)(2,1)S(1)} collective-permute-done((bf16[1024,128]{1,0:T(8,128)(2,1)S(1)}, bf16[1024,128]{1,0:T(8,128)(2,1)S(1)}, u32[]{:S(2)}, u32[]{:S(2)}) %collective-permute-start.2) | collective-permute-done | bytes 262176 | tf_op jit(solution)/shard_map/ppermute | solution.py:738
  33.9 6.1 %cross_open.1 = (bf16[2048,128]{1,0:T(8,128)(2,1)S(1)}, bf16[2048,128]{1,0:T(8,128)(2,1)S(1)}, bf16[1024,256]{1,0:T(8,128)(2,1)S(1)}, f32[128,2048]{1,0:T(8,128)...) custom-call(bf16[1024,128]{1,0:T(8,128)(2,1)S(1)} %get-tuple-element.64.low_ref, ...), custom_call_target="tpu_custom_call" | custom-call | tf_op jit(solution)/shard_map/cross_open/pallas_call | solution.py:219
  40.0 0.0 collective-permute-done.3.partner_ref.refs_5_
  40.0 13.4 %cross_close.1 = (bf16[1024,256]{1,0:T(8,128)(2,1)S(1)}, bf16[2048,128]{1,0:T(8,128)(2,1)}, f32[2048,128]{1,0:T(8,128)S(1)}, bf16[2048,128]{1,0:T(8,128)(2,1)S(1...) custom-call(bf16[2048,128]{1,0:T(8,128)(2,1)S(1)} %get-tuple-element, ...), custom_call_target="tpu_custom_call" | custom-call | tf_op jit(solution)/shard_map/cross_close/pallas_call | solution.py:354
  53.5 4.4 %cross_back.4 = (bf16[512,128]{1,0:T(8,128)(2,1)S(1)}, f32[2048,128]{1,0:T(8,128)S(1)}, f32[3,128,128]{2,1,0:T(8,128)S(1)}) custom-call(bf16[2048,128]{1,0:T(8,128)(2,1)S(1)} %get-tuple-element.67.q_ref.refs_0_, bf16[2048,128]{1,0:T(8,128)(2,1)S(1)} %get-tuple-element.74.refs_1_, f32[8,2048]{1,0:T(8,128)S(1)} %get-tuple-element.75.refs_2_, ...), custom_call_target="tpu_custom_call" | custom-call | tf_op jit(solution)/shard_map/cross_back/pallas_call | solution.py:467
  57.8 0.1 collective-permute-start.4
  57.9 4.4 %cross_back.5 = (bf16[512,128]{1,0:T(8,128)(2,1)S(1)}, f32[2048,128]{1,0:T(8,128)S(1)}, f32[3,128,128]{2,1,0:T(8,128)S(1)}) custom-call(bf16[2048,128]{1,0:T(8,128)(2,1)S(1)} %get-tuple-element.67.q_ref.refs_0_, bf16[2048,128]{1,0:T(8,128)(2,1)S(1)} %get-tuple-element.74.refs_1_, f32[8,2048]{1,0:T(8,128)S(1)} %get-tuple-element.75.refs_2_, ...), custom_call_target="tpu_custom_call" | custom-call | tf_op jit(solution)/shard_map/cross_back/pallas_call | solution.py:467
  62.3 3.0 %collective-permute-start.5 = (bf16[512,128]{1,0:T(8,128)(2,1)S(1)}, bf16[512,128]{1,0:T(8,128)(2,1)S(1)}, u32[]{:S(2)}, u32[]{:S(2)}) collective-permute-start(bf16[512,128]{1,0:T(8,128)(2,1)S(1)} %get-tuple-element.89), channel_id=1, source_target_pairs={{0,8},{1,9},{2,10},{3,11},{4,12},{5,13},{6,14},{7,15},{8,0},{9,1},... | collective-permute-start | bytes 393224 | tf_op jit(solution)/shard_map/ppermute | solution.py:762
  65.2 4.4 %cross_back.6 = (bf16[512,128]{1,0:T(8,128)(2,1)S(1)}, f32[2048,128]{1,0:T(8,128)S(1)}, f32[3,128,128]{2,1,0:T(8,128)S(1)}) custom-call(bf16[2048,128]{1,0:T(8,128)(2,1)S(1)} %get-tuple-element.67.q_ref.refs_0_, bf16[2048,128]{1,0:T(8,128)(2,1)S(1)} %get-tuple-element.74.refs_1_, f32[8,2048]{1,0:T(8,128)S(1)} %get-tuple-element.75.refs_2_, ...), custom_call_target="tpu_custom_call" | custom-call | tf_op jit(solution)/shard_map/cross_back/pallas_call | solution.py:467
  69.6 4.9 %cross_back.7 = (bf16[512,128]{1,0:T(8,128)(2,1)S(1)}, f32[2048,128]{1,0:T(8,128)S(1)}, f32[3,128,128]{2,1,0:T(8,128)S(1)}) custom-call(bf16[2048,128]{1,0:T(8,128)(2,1)S(1)} %get-tuple-element.67.q_ref.refs_0_, bf16[2048,128]{1,0:T(8,128)(2,1)S(1)} %get-tuple-element.74.refs_1_, f32[8,2048]{1,0:T(8,128)S(1)} %get-tuple-element.75.refs_2_, ...), custom_call_target="tpu_custom_call" | custom-call | tf_op jit(solution)/shard_map/cross_back/pallas_call | solution.py:467
  74.5 0.0 collective-permute-done.4.term_low_ref
  74.5 0.0 collective-permute-done.5.term_high_ref
  74.5 5.8 %self_back.2 = (f32[1024,128]{1,0:T(8,128)S(1)}, bf16[1024,128]{1,0:T(8,128)(2,1)S(1)}, f32[3,128,128]{2,1,0:T(8,128)S(1)}, f32[128,128]{1,0:T(8,128)S(1)}, f32[8,128]{1,0:T(8,128)S(1)}) custom-call(s32[2]{0:T(128)S(1)} %copy-done, s32[1]{0:T(128)} %bitcast.place_ref, bf16[16,128,128]{2,1,0:T(8,128)(2,1)} %own_ref.7, ...), custom_call_target="tpu_custom_call" | custom-call | tf_op jit(solution)/shard_map/self_back/pallas_call | solution.py:567
  80.3 2.9 %collective-permute-start.9 = (bf16[1024,128]{1,0:T(8,128)(2,1)S(1)}, bf16[1024,128]{1,0:T(8,128)(2,1)S(1)}, u32[]{:S(2)}, u32[]{:S(2)}) collective-permute-start(bf16[1024,128]{1,0:T(8,128)(2,1)S(1)} %get-tuple-element.98), channel_id=1, source_target_pairs={{5,4},{6,5},{7,6},{8,7},{9,8},{10,9},{11,10},{13,12},{14,13},{15,1... | collective-permute-start | bytes 786440 | tf_op jit(solution)/shard_map/ppermute | solution.py:774
  83.2 0.1 collective-permute-start.6
  83.3 2.9 %collective-permute-start.7 = (bf16[512,128]{1,0:T(8,128)(2,1)S(1)}, bf16[512,128]{1,0:T(8,128)(2,1)S(1)}, u32[]{:S(2)}, u32[]{:S(2)}) collective-permute-start(bf16[512,128]{1,0:T(8,128)(2,1)S(1)} %get-tuple-element.95), channel_id=1, source_target_pairs={{0,8},{1,9},{2,10},{3,11},{4,12},{5,13},{6,14},{7,15},{8,0},{9,1},... | collective-permute-start | bytes 393224 | tf_op jit(solution)/shard_map/ppermute | solution.py:762
  86.2 9.2 %collective-permute-done.6.term_low_ref = bf16[512,128]{1,0:T(8,128)(2,1)S(1)} collective-permute-done((bf16[512,128]{1,0:T(8,128)(2,1)S(1)}, bf16[512,128]{1,0:T(8,128)(2,1)S(1)}, u32[]{:S(2)}, u32[]{:S(2)}) %collective-permute-start.6) | collective-permute-done | bytes 131104 | tf_op jit(solution)/shard_map/ppermute | solution.py:762
  95.4 1.4 %collective-permute-done.7.term_high_ref = bf16[512,128]{1,0:T(8,128)(2,1)S(1)} collective-permute-done((bf16[512,128]{1,0:T(8,128)(2,1)S(1)}, bf16[512,128]{1,0:T(8,128)(2,1)S(1)}, u32[]{:S(2)}, u32[]{:S(2)}) %collective-permute-start.7) | collective-permute-done | bytes 131104 | tf_op jit(solution)/shard_map/ppermute | solution.py:762
  96.8 5.8 %self_back.3 = (f32[1024,128]{1,0:T(8,128)S(1)}, bf16[1024,128]{1,0:T(8,128)(2,1)S(1)}, f32[3,128,128]{2,1,0:T(8,128)S(1)}, f32[128,128]{1,0:T(8,128)S(1)}, f32[8,128]{1,0:T(8,128)S(1)}) custom-call(s32[2]{0:T(128)S(1)} %copy-done, s32[1]{0:T(128)} %bitcast.place_ref, bf16[16,128,128]{2,1,0:T(8,128)(2,1)} %own_ref.7, ...), custom_call_target="tpu_custom_call" | custom-call | tf_op jit(solution)/shard_map/self_back/pallas_call | solution.py:567
  102.6 0.1 pack.1
  102.8 0.1 collective-permute-start.10
  102.9 2.4 %collective-permute-start.8 = (bf16[1024,128]{1,0:T(8,128)(2,1)S(1)}, bf16[1024,128]{1,0:T(8,128)(2,1)S(1)}, u32[]{:S(2)}, u32[]{:S(2)}) collective-permute-start(bf16[1024,128]{1,0:T(8,128)(2,1)S(1)} %get-tuple-element.96), channel_id=1, source_target_pairs={{4,5},{5,6},{6,7},{7,8},{8,9},{9,10},{10,11},{12,13},{13,14},{14,1... | collective-permute-start | bytes 786440 | tf_op jit(solution)/shard_map/ppermute | solution.py:774
  105.3 0.0 collective-permute-done.9
  105.3 0.0 collective-permute-done.10
  105.3 0.1 convert_add_fusion
  105.4 3.7 %collective-permute-start.11 = (bf16[4,168,128]{2,1,0:T(8,128)(2,1)S(1)}, bf16[4,168,128]{2,1,0:T(8,128)(2,1)S(1)}, u32[]{:S(2)}, u32[]{:S(2)}) collective-permute-start(bf16[4,168,128]{2,1,0:T(8,128)(2,1)S(1)} %fusion), channel_id=1, source_target_pairs={{0,2},{1,3},{2,0},{3,1},{4,6},{5,7},{6,4},{7,5},{8,10},{9,11},{10,... | collective-permute-start | bytes 516104 | tf_op jit(solution)/shard_map/ppermute | solution.py:690
  109.2 5.1 %collective-permute-done.8 = bf16[1024,128]{1,0:T(8,128)(2,1)S(1)} collective-permute-done((bf16[1024,128]{1,0:T(8,128)(2,1)S(1)}, bf16[1024,128]{1,0:T(8,128)(2,1)S(1)}, u32[]{:S(2)}, u32[]{:S(2)}) %collective-permute-start.8) | collective-permute-done | bytes 262176 | tf_op jit(solution)/shard_map/ppermute | solution.py:774
  114.3 2.2 %collective-permute-done.11 = bf16[4,168,128]{2,1,0:T(8,128)(2,1)S(1)} collective-permute-done((bf16[4,168,128]{2,1,0:T(8,128)(2,1)S(1)}, bf16[4,168,128]{2,1,0:T(8,128)(2,1)S(1)}, u32[]{:S(2)}, u32[]{:S(2)}) %collective-permute-start.11) | collective-permute-done | bytes 172064 | tf_op jit(solution)/shard_map/ppermute | solution.py:690
  116.5 0.1 bitcast_add_fusion
  116.6 0.1 collective-permute-start.12
  116.6 1.0 pad_maximum_fusion
  117.7 3.9 %collective-permute-done.12 = bf16[2,168,128]{2,1,0:T(8,128)(2,1)S(1)} collective-permute-done((bf16[2,168,128]{2,1,0:T(8,128)(2,1)S(1)}, bf16[2,168,128]{2,1,0:T(8,128)(2,1)S(1)}, u32[]{:S(2)}, u32[]{:S(2)}) %collective-permute-start.12) | collective-permute-done | bytes 86048 | tf_op jit(solution)/shard_map/ppermute | solution.py:690
  121.7 0.1 collective-permute-start.13
  121.8 5.1 %collective-permute-done.13.got_ref = bf16[1,168,128]{2,1,0:T(8,128)(2,1)S(1)} collective-permute-done((bf16[1,168,128]{2,1,0:T(8,128)(2,1)S(1)}, bf16[1,168,128]{2,1,0:T(8,128)(2,1)S(1)}, u32[]{:S(2)}, u32[]{:S(2)}) %collective-permute-start.13) | collective-permute-done | bytes 43040 | tf_op jit(solution)/shard_map/ppermute | solution.py:690
  126.8 0.7 unpack.1
  (7 shorter events, 0.2 us)
Async XLA Ops:
  1.7 11.5 %collective-permute-start = (bf16[8,128,128]{2,1,0:T(8,128)(2,1)S(1)}, bf16[8,128,128]{2,1,0:T(8,128)(2,1)S(1)}, u32[]{:S(2)}, u32[]{:S(2)}) collective-permute-start(bf16[8,128,128]{2,1,0:T(8,128)(2,1)S(1)} %get-tuple-element.120), channel_id=1, source_target_pairs={{4,5},{5,6},{6,7},{7,8},{8,9},{9,10},{10,11},{12,13},{13,14},{14,1... | collective-permute-start | bytes 786440 | tf_op jit(solution)/shard_map/ppermute | solution.py:731
  4.1 15.2 %collective-permute-start.1 = (bf16[8,128,128]{2,1,0:T(8,128)(2,1)S(1)}, bf16[8,128,128]{2,1,0:T(8,128)(2,1)S(1)}, u32[]{:S(2)}, u32[]{:S(2)}) collective-permute-start(bf16[8,128,128]{2,1,0:T(8,128)(2,1)S(1)} %get-tuple-element.119), channel_id=1, source_target_pairs={{5,4},{6,5},{7,6},{8,7},{9,8},{10,9},{11,10},{13,12},{14,13},{15,1... | collective-permute-start | bytes 786440 | tf_op jit(solution)/shard_map/ppermute | solution.py:732
  13.2 0.7 copy-start
  18.1 15.8 %collective-permute-start.2 = (bf16[1024,128]{1,0:T(8,128)(2,1)S(1)}, bf16[1024,128]{1,0:T(8,128)(2,1)S(1)}, u32[]{:S(2)}, u32[]{:S(2)}) collective-permute-start(bf16[1024,128]{1,0:T(8,128)(2,1)S(1)} %get-tuple-element.64.low_ref), channel_id=1, source_target_pairs={{0,8},{1,9},{2,10},{3,11},{4,12},{5,13},{6,14},{7,15},{8,0},{9,1},... | collective-permute-start | bytes 786440 | tf_op jit(solution)/shard_map/ppermute | solution.py:738
  23.5 16.5 %collective-permute-start.3 = (bf16[1024,128]{1,0:T(8,128)(2,1)S(1)}, bf16[1024,128]{1,0:T(8,128)(2,1)S(1)}, u32[]{:S(2)}, u32[]{:S(2)}) collective-permute-start(bf16[1024,128]{1,0:T(8,128)(2,1)S(1)} %get-tuple-element.65.high_ref), channel_id=1, source_target_pairs={{0,8},{1,9},{2,10},{3,11},{4,12},{5,13},{6,14},{7,15},{8,0},{9,1},... | collective-permute-start | bytes 786440 | tf_op jit(solution)/shard_map/ppermute | solution.py:738
  57.8 16.6 %collective-permute-start.4 = (bf16[512,128]{1,0:T(8,128)(2,1)S(1)}, bf16[512,128]{1,0:T(8,128)(2,1)S(1)}, u32[]{:S(2)}, u32[]{:S(2)}) collective-permute-start(bf16[512,128]{1,0:T(8,128)(2,1)S(1)} %get-tuple-element.88), channel_id=1, source_target_pairs={{0,8},{1,9},{2,10},{3,11},{4,12},{5,13},{6,14},{7,15},{8,0},{9,1},... | collective-permute-start | bytes 393224 | tf_op jit(solution)/shard_map/ppermute | solution.py:762
  62.3 12.2 %collective-permute-start.5 = (bf16[512,128]{1,0:T(8,128)(2,1)S(1)}, bf16[512,128]{1,0:T(8,128)(2,1)S(1)}, u32[]{:S(2)}, u32[]{:S(2)}) collective-permute-start(bf16[512,128]{1,0:T(8,128)(2,1)S(1)} %get-tuple-element.89), channel_id=1, source_target_pairs={{0,8},{1,9},{2,10},{3,11},{4,12},{5,13},{6,14},{7,15},{8,0},{9,1},... | collective-permute-start | bytes 393224 | tf_op jit(solution)/shard_map/ppermute | solution.py:762
  80.3 24.9 %collective-permute-start.9 = (bf16[1024,128]{1,0:T(8,128)(2,1)S(1)}, bf16[1024,128]{1,0:T(8,128)(2,1)S(1)}, u32[]{:S(2)}, u32[]{:S(2)}) collective-permute-start(bf16[1024,128]{1,0:T(8,128)(2,1)S(1)} %get-tuple-element.98), channel_id=1, source_target_pairs={{5,4},{6,5},{7,6},{8,7},{9,8},{10,9},{11,10},{13,12},{14,13},{15,1... | collective-permute-start | bytes 786440 | tf_op jit(solution)/shard_map/ppermute | solution.py:774
  83.2 12.2 %collective-permute-start.6 = (bf16[512,128]{1,0:T(8,128)(2,1)S(1)}, bf16[512,128]{1,0:T(8,128)(2,1)S(1)}, u32[]{:S(2)}, u32[]{:S(2)}) collective-permute-start(bf16[512,128]{1,0:T(8,128)(2,1)S(1)} %get-tuple-element.94), channel_id=1, source_target_pairs={{0,8},{1,9},{2,10},{3,11},{4,12},{5,13},{6,14},{7,15},{8,0},{9,1},... | collective-permute-start | bytes 393224 | tf_op jit(solution)/shard_map/ppermute | solution.py:762
  83.3 13.5 %collective-permute-start.7 = (bf16[512,128]{1,0:T(8,128)(2,1)S(1)}, bf16[512,128]{1,0:T(8,128)(2,1)S(1)}, u32[]{:S(2)}, u32[]{:S(2)}) collective-permute-start(bf16[512,128]{1,0:T(8,128)(2,1)S(1)} %get-tuple-element.95), channel_id=1, source_target_pairs={{0,8},{1,9},{2,10},{3,11},{4,12},{5,13},{6,14},{7,15},{8,0},{9,1},... | collective-permute-start | bytes 393224 | tf_op jit(solution)/shard_map/ppermute | solution.py:762
  102.8 2.5 %collective-permute-start.10 = (bf16[8,168,128]{2,1,0:T(8,128)(2,1)S(1)}, bf16[8,168,128]{2,1,0:T(8,128)(2,1)S(1)}, u32[]{:S(2)}, u32[]{:S(2)}) collective-permute-start(bf16[8,168,128]{2,1,0:T(8,128)(2,1)S(1)} %get-tuple-element.111), channel_id=1, source_target_pairs={{0,1},{1,0},{2,3},{3,2},{4,5},{5,4},{6,7},{7,6},{8,9},{9,8},{10,11... | collective-permute-start | bytes 1032200 | tf_op jit(solution)/shard_map/ppermute | solution.py:690
  102.9 11.4 %collective-permute-start.8 = (bf16[1024,128]{1,0:T(8,128)(2,1)S(1)}, bf16[1024,128]{1,0:T(8,128)(2,1)S(1)}, u32[]{:S(2)}, u32[]{:S(2)}) collective-permute-start(bf16[1024,128]{1,0:T(8,128)(2,1)S(1)} %get-tuple-element.96), channel_id=1, source_target_pairs={{4,5},{5,6},{6,7},{7,8},{8,9},{9,10},{10,11},{12,13},{13,14},{14,1... | collective-permute-start | bytes 786440 | tf_op jit(solution)/shard_map/ppermute | solution.py:774
  105.4 11.0 %collective-permute-start.11 = (bf16[4,168,128]{2,1,0:T(8,128)(2,1)S(1)}, bf16[4,168,128]{2,1,0:T(8,128)(2,1)S(1)}, u32[]{:S(2)}, u32[]{:S(2)}) collective-permute-start(bf16[4,168,128]{2,1,0:T(8,128)(2,1)S(1)} %fusion), channel_id=1, source_target_pairs={{0,2},{1,3},{2,0},{3,1},{4,6},{5,7},{6,4},{7,5},{8,10},{9,11},{10,... | collective-permute-start | bytes 516104 | tf_op jit(solution)/shard_map/ppermute | solution.py:690
  116.6 5.1 %collective-permute-start.12 = (bf16[2,168,128]{2,1,0:T(8,128)(2,1)S(1)}, bf16[2,168,128]{2,1,0:T(8,128)(2,1)S(1)}, u32[]{:S(2)}, u32[]{:S(2)}) collective-permute-start(bf16[2,168,128]{2,1,0:T(8,128)(2,1)S(1)} %fusion.2), channel_id=1, source_target_pairs={{0,4},{1,5},{2,6},{3,7},{4,0},{5,1},{6,2},{7,3},{8,12},{9,13},{10,... | collective-permute-start | bytes 258056 | tf_op jit(solution)/shard_map/ppermute | solution.py:690
  121.7 5.2 %collective-permute-start.13 = (bf16[1,168,128]{2,1,0:T(8,128)(2,1)S(1)}, bf16[1,168,128]{2,1,0:T(8,128)(2,1)S(1)}, u32[]{:S(2)}, u32[]{:S(2)}) collective-permute-start(bf16[1,168,128]{2,1,0:T(8,128)(2,1)S(1)} %fusion.3), channel_id=1, source_target_pairs={{0,8},{1,9},{2,10},{3,11},{4,12},{5,13},{6,14},{7,15},{8,0},{9,1},... | collective-permute-start | bytes 129032 | tf_op jit(solution)/shard_map/ppermute | solution.py:690
